TPU v7x, 32 devices: a whole 2x2x4 slice. The times are simulated.
32 devices in a mesh: cell: 16 (over z, y, core), dir: 2 (over x).
Axes of the slice: x: 2, y: 2, z: 4, core: 2. Of those that a mesh axis runs over, the one named last changes fastest.
Arguments:
- atom_features: bfloat16 [512, 128, 128], P('cell'), may hold values from -6 to 6
- positions: bfloat16 [512, 3, 128], P('cell'), may hold values from 0 to 12
- neighbours: int32 [512, 4], P('cell'), may hold values from 0 to 39, as said below
- counts: int32 [16], replicated, may hold values from 4 to 28, as said below
- filter_gains: float32 [8, 128], replicated, may hold values from -0.25 to 0.25
- w_update: bfloat16 [128, 128], replicated, may hold values from -0.5 to 0.5
- projections: bfloat16 [128, 384], replicated, may hold values from -0.5 to 0.5
- w_output: bfloat16 [128, 128], replicated, may hold values from -0.5 to 0.5
Outputs:
- attended: bfloat16 [256, 128, 128], P(('cell', 'dir'))
Inputs may be any that keep to these rules, and one draw needn't show every extreme that they name: counts[c] live slots (slots 0 to counts[c] - 1) in cell c; the counts sum to 256; some cell holds the least and some the most. `neighbours`: for a live slot of cell c every entry is below 4 (a face block of the cell before), or from 4 to 4 + counts[c] - 1 (a live block of c), or 36 or more (a face block of the cell after); entries of dead slots lie in the same range.
All inputs are finite; a program needn't handle non-finite values.
Results may differ from a plain program's by a relative error of at most 0.014.
Values may be sent and summed in bfloat16 or wider, within the bound.
A program may use at most 128 MiB of HBM per device.

v0:
```python
import functools
import math

import jax
import jax.numpy as jnp
import numpy as np
from jax import lax
from jax.experimental import pallas as pl
from jax.experimental.pallas import tpu as pltpu
from jax.sharding import PartitionSpec as P

DIRS = 50
H = 4


slab_width = 12.0
radial_width = 0.6
golden_turn = math.pi * (3.0 - math.sqrt(5.0))


def shift_component(positions_in, amount):
    marker = (jnp.arange(positions_in.shape[-2]) == 0).astype(jnp.float32)
    return positions_in + amount * marker[:, None]


def direction_rows(total, shares):
    order = np.arange(total, dtype=np.float64)
    height = 1.0 - (2.0 * order + 1.0) / total
    radius = np.sqrt(1.0 - height * height)
    turning = order * golden_turn
    share = total // shares
    table = np.zeros((shares, -(-share // 8) * 8, 128), np.float32)
    unit = np.stack([radius * np.cos(turning), radius * np.sin(turning), height], axis=1)
    table[:, :share, :3] = unit.reshape(shares, share, 3)
    return table


def directions_per_turn(share):
    return max(g for g in range(1, 6) if share % g == 0)


def store_powers(table, coords, half, cosines, sines):
    base = (
        table[:, 0:1] * coords[0:1] + table[:, 1:2] * coords[1:2] + table[:, 2:3] * coords[2:3]
    ) * (0.5 / half)
    count = table.shape[0]
    c1, s1 = jnp.cos(base), jnp.sin(base)
    powers = {1: (c1, s1)}
    for n in range(2, 9):
        (ca, sa), (cb, sb) = powers[n // 2], powers[n - n // 2]
        powers[n] = (ca * cb - sa * sb, sa * cb + ca * sb)
    for n in range(1, 9):
        for tile in range(base.shape[1] // 128):
            lanes = slice(tile * 128, (tile + 1) * 128)
            cosines[tile, (n - 1) * count : n * count, :] = powers[n][0][:, lanes]
            sines[tile, (n - 1) * count : n * count, :] = powers[n][1][:, lanes]


def rotated(features, direction, count, half, cosines, sines):
    rows = pl.ds(direction, 8, stride=count)
    last = pl.ds(7 * count + direction, 1)

    def across(held, at):
        return jnp.concatenate([held[tile, at, :] for tile in range(held.shape[0])], axis=1)

    cosine, sine = across(cosines, rows), across(sines, rows)
    step_c = jnp.broadcast_to(across(cosines, last), cosine.shape)
    step_s = jnp.broadcast_to(across(sines, last), sine.shape)
    double = 2.0 * step_c
    older = None
    turned = []
    for first in range(0, half, 8):
        if first == 8:
            older = (cosine, sine)
            cosine, sine = cosine * step_c - sine * step_s, sine * step_c + cosine * step_s
        elif first > 8:
            held = (cosine, sine)
            cosine, sine = double * cosine - older[0], double * sine - older[1]
            older = held
        turned.append((cosine, sine))
    low, high = [], []
    for first in range(0, half, 16):
        pair = turned[first // 8 : first // 8 + 2]
        cosine, sine = [
            jnp.concatenate([both[which] for both in pair], axis=0).astype(jnp.bfloat16)
            for which in range(2)
        ]
        a = features[first : first + 16, :]
        b = features[half + first : half + first + 16, :]
        low.append(a * cosine - b * sine)
        high.append(b * cosine + a * sine)
    return [jnp.concatenate(low + high, axis=0)]


def kv_kernel(chunk, share, live_ref, table_ref, coords_ref, rows_ref, weights_t_ref, weights_ref, out_ref, states_ref, keys, cosines, sines):
    width = rows_ref.shape[1]
    half = width // 2
    count = table_ref.shape[0]
    per_turn = directions_per_turn(share)
    states_ref[...] = jnp.zeros_like(states_ref)
    live = live_ref[0]

    def advance(turn, carried):
        at = pl.ds(pl.multiple_of(turn * chunk, chunk), chunk)
        rows = rows_ref[at, :]
        keys[...] = lax.dot_general(
            weights_t_ref[width : 2 * width, :], rows, (((1,), (1,)), ((), ())),
            preferred_element_type=jnp.float32,
        ).astype(jnp.bfloat16)
        values = jnp.dot(rows, weights_ref[:, 2 * width :], preferred_element_type=jnp.float32)
        index = turn * chunk + lax.broadcasted_iota(jnp.int32, values.shape, 0)
        values = jnp.where(index < live, values, 0.0).astype(jnp.bfloat16)
        store_powers(table_ref[...], coords_ref[:, at], half, cosines, sines)

        for group in range(share // per_turn):
            parts = []
            for j in range(per_turn):
                parts += rotated(keys, group * per_turn + j, count, half, cosines, sines)
            size = per_turn * width
            states_ref[group * size : (group + 1) * size, :] += jnp.dot(
                jnp.concatenate(parts, axis=0), values, preferred_element_type=jnp.float32
            )
        return carried

    lax.fori_loop(0, (live + chunk - 1) // chunk, advance, 0)
    out_ref[...] = states_ref[...].astype(out_ref.dtype)


def query_kernel(chunk, share, table_ref, coords_ref, rows_ref, weights_t_ref, states_ref, out_ref, queries, flipped, cosines, sines):
    atoms, width = rows_ref.shape
    half = width // 2
    count = table_ref.shape[0]
    per_turn = directions_per_turn(share)
    for d in range(share):
        flipped[:, d * width : (d + 1) * width] = states_ref[d * width : (d + 1) * width, :].T

    def advance(turn, carried):
        at = pl.ds(pl.multiple_of(turn * chunk, chunk), chunk)
        queries[...] = lax.dot_general(
            weights_t_ref[:width, :], rows_ref[at, :], (((1,), (1,)), ((), ())),
            preferred_element_type=jnp.float32,
        ).astype(jnp.bfloat16)
        store_powers(table_ref[...], coords_ref[:, at], half, cosines, sines)
        summed = None
        for group in range(share // per_turn):
            parts = []
            for j in range(per_turn):
                parts += rotated(queries, group * per_turn + j, count, half, cosines, sines)
            size = per_turn * width
            term = jnp.dot(
                flipped[:, group * size : (group + 1) * size], jnp.concatenate(parts, axis=0),
                preferred_element_type=jnp.float32,
            )
            summed = term if summed is None else summed + term
        out_ref[at, :] = summed.T
        return carried

    lax.fori_loop(0, atoms // chunk, advance, 0)


def vmem(count):
    return [pl.BlockSpec(memory_space=pltpu.VMEM)] * count


def kv_states(live, table, coords, flat, weights_t, weights, share, padded_rows, dtype):
    width = flat.shape[1]
    chunk = 256
    count = table.shape[0]
    atoms = flat.shape[0] // 2
    return pl.pallas_call(
        functools.partial(kv_kernel, chunk, share),
        out_shape=jax.ShapeDtypeStruct((padded_rows, width), dtype),
        in_specs=[pl.BlockSpec(memory_space=pltpu.SMEM)] + vmem(5),
        out_specs=pl.BlockSpec(memory_space=pltpu.VMEM),
        scratch_shapes=[
            pltpu.VMEM((padded_rows, width), jnp.float32),
            pltpu.VMEM((width, chunk), jnp.bfloat16),
            pltpu.VMEM((chunk // 128, 8 * count, 128), jnp.float32),
            pltpu.VMEM((chunk // 128, 8 * count, 128), jnp.float32),
        ],
        cost_estimate=pl.CostEstimate(
            flops=2 * share * atoms * width * width * 8, bytes_accessed=20_000_000, transcendentals=0
        ),
        name="kv_states",
    )(live, table, coords, flat, weights_t, weights)


def query_mix(table, coords, flat, weights_t, states, share):
    atoms, width = flat.shape
    chunk = 256
    count = table.shape[0]
    return pl.pallas_call(
        functools.partial(query_kernel, chunk, share),
        out_shape=jax.ShapeDtypeStruct((atoms, width), jnp.float32),
        in_specs=vmem(5),
        out_specs=pl.BlockSpec(memory_space=pltpu.VMEM),
        scratch_shapes=[
            pltpu.VMEM((width, chunk), jnp.bfloat16),
            pltpu.VMEM((width, share * width), jnp.bfloat16),
            pltpu.VMEM((chunk // 128, 8 * count, 128), jnp.float32),
            pltpu.VMEM((chunk // 128, 8 * count, 128), jnp.float32),
        ],
        cost_estimate=pl.CostEstimate(
            flops=2 * share * atoms * width * width * 8, bytes_accessed=20_000_000, transcendentals=0
        ),
        name="query_mix",
    )(table, coords, flat, weights_t, states)


def reduce_orders(bits):
    first = list(range(bits))
    second = list(first)
    if bits > 2:
        second[1], second[2] = second[2], second[1]
    return [first, second, first, second]


def piece_rows(rows, unit, pieces):
    units = rows // unit
    return [(units // pieces + (k < units % pieces)) * unit for k in range(pieces)]


def reduce_kernel(bits, local_ref, away_ref, out_ref, total, sent, landed, turned, crossed, arrived, send_sems, recv_sems, gather_send, gather_recv, cross_send, cross_recv):
    me = lax.axis_index("cell")

    def bit_of(b):
        return lax.rem(me // (1 << b), 2)

    def partner(b):
        return {"cell": me + (1 - 2 * bit_of(b)) * (1 << b)}

    barrier = pltpu.get_barrier_semaphore()
    for b in range(bits):
        pl.semaphore_signal(
            barrier, inc=1, device_id=partner(b), device_id_type=pl.DeviceIdType.MESH
        )
    other = {"dir": 1 - lax.axis_index("dir")}
    pl.semaphore_signal(barrier, inc=1, device_id=other, device_id_type=pl.DeviceIdType.MESH)
    orders = reduce_orders(bits)
    lengths = piece_rows(local_ref.shape[0], 16 * (1 << bits), len(orders))
    starts = [sum(lengths[:k]) for k in range(len(orders))]
    offsets = list(starts)

    def own(step, at):
        return local_ref[at, :] if step == 0 else total[at, :]

    pieces = range(len(orders))
    running = {}

    def copy_to(device, source, target, send_sem, recv_sem):
        copy = pltpu.make_async_remote_copy(
            src_ref=source,
            dst_ref=target,
            send_sem=send_sem,
            recv_sem=recv_sem,
            device_id=device,
            device_id_type=pl.DeviceIdType.MESH,
        )
        copy.start()
        return copy

    def issue(k, stage):
        if stage < bits:
            b, half = orders[k][stage], lengths[k] // 2
            away = pl.multiple_of(starts[k] + (1 - bit_of(b)) * half, 16)
            at = pl.ds(offsets[k], half)
            sent[at, :] = own(stage, pl.ds(away, half)).astype(jnp.bfloat16)
            if stage == 0 and k == 0:
                pl.semaphore_wait(barrier, bits + 1)
            if stage == 0:
                turned[at, :] = away_ref[pl.ds(away, half), :]
                running[k, "turned"] = copy_to(
                    partner(b), turned.at[at, :], crossed.at[at, :], cross_send.at[k, 0], cross_recv.at[k, 0]
                )
            running[k, stage] = copy_to(
                partner(b), sent.at[at, :], landed.at[at, :], send_sems.at[k, stage], recv_sems.at[k, stage]
            )
        else:
            step = 2 * bits - 1 - stage
            at = pl.ds(pl.multiple_of(starts[k], 16), lengths[k])
            running[k, stage] = copy_to(
                partner(orders[k][step]), out_ref.at[at, :], out_ref.at[at, :],
                gather_send.at[k, step], gather_recv.at[k, step],
            )

    def finish(k, stage):
        running[k, stage].wait_recv()
        if stage < bits:
            half = lengths[k] // 2
            keep = pl.multiple_of(starts[k] + bit_of(orders[k][stage]) * half, 16)
            at = pl.ds(offsets[k], half)
            summed = own(stage, pl.ds(keep, half)) + landed[at, :].astype(jnp.float32)
            if stage == bits - 1:
                out_ref[pl.ds(keep, half), :] = summed.astype(jnp.bfloat16)
            else:
                total[pl.ds(keep, half), :] = summed
            if stage == 0:
                running[k, "turned"].wait_recv()
                rest = pl.ds(offsets[k] + half, half)
                turned[rest, :] = (
                    away_ref[pl.ds(keep, half), :].astype(jnp.float32) + crossed[at, :].astype(jnp.float32)
                ).astype(jnp.bfloat16)
                running[k, "across"] = copy_to(
                    other, turned.at[rest, :], arrived.at[rest, :], cross_send.at[k, 1], cross_recv.at[k, 1]
                )
            starts[k], lengths[k] = keep, half
            offsets[k] += half
        else:
            step = 2 * bits - 1 - stage
            starts[k] = starts[k] - bit_of(orders[k][step]) * lengths[k]
            lengths[k] = 2 * lengths[k]

    def absorb(k):
        running[k, "across"].wait_recv()
        held = pl.ds(pl.multiple_of(starts[k], 16), lengths[k])
        came = arrived[pl.ds(offsets[k], lengths[k]), :]
        total[held, :] = total[held, :] + came.astype(jnp.float32)

    for k in pieces:
        issue(k, 0)
    for k in pieces:
        finish(k, 0)
    for stage in range(1, 2 * bits + 1):
        for k in pieces:
            if stage == 1:
                absorb(k)
            else:
                finish(k, stage - 1)
            if stage < 2 * bits:
                issue(k, stage)
    for copy in running.values():
        copy.wait_send()


def reduce_states(local, away, cells):
    bits = cells.bit_length() - 1
    rows, width = local.shape
    pieces = len(reduce_orders(bits))
    return pl.pallas_call(
        functools.partial(reduce_kernel, bits),
        out_shape=jax.ShapeDtypeStruct((rows, width), jnp.bfloat16),
        in_specs=vmem(2),
        out_specs=pl.BlockSpec(memory_space=pltpu.VMEM),
        scratch_shapes=[
            pltpu.VMEM((rows, width), jnp.float32),
        ]
        + [pltpu.VMEM((rows, width), jnp.bfloat16)] * 5
        + [pltpu.SemaphoreType.DMA((pieces, bits))] * 4
        + [pltpu.SemaphoreType.DMA((pieces, 2))] * 2,
        compiler_params=pltpu.CompilerParams(collective_id=0, has_side_effects=True),
        cost_estimate=pl.CostEstimate(flops=20_000_000_000, bytes_accessed=60_000_000, transcendentals=0),
        name="reduce_states",
    )(local, away)


def radial_terms(own_positions, near_positions, near_features, filter_gains):
    differ = own_positions[:, None, :, :, None] - near_positions[:, :, :, None, :]
    distance = jnp.sqrt(jnp.sum(differ * differ, axis=2))
    centers = 2.0 + 2.0 * jnp.arange(filter_gains.shape[0], dtype=jnp.float32)
    scaled = (distance[:, :, None] - centers[None, None, :, None, None]) / radial_width
    radial = jnp.exp(-scaled * scaled).astype(jnp.bfloat16)
    summed = jnp.einsum(
        "gnkab,gnbf->gkaf", radial, near_features, preferred_element_type=jnp.float32
    )
    return jnp.sum(summed * filter_gains[None, :, None, :], axis=1)


def block_messages(live_count, group_width, picks, own_positions, extended_features, extended_positions, filter_gains):
    slot_count = picks.shape[0]
    initial = jnp.zeros(
        (slot_count, extended_features.shape[1], extended_features.shape[2]), jnp.float32
    )

    def block_advance(turn_index, running):
        at = turn_index * group_width
        picked = lax.dynamic_slice_in_dim(picks, at, group_width, 0)
        near_features = extended_features[picked]
        near_positions = extended_positions[picked]
        own = lax.dynamic_slice_in_dim(own_positions, at, group_width, 0)
        result = radial_terms(own, near_positions, near_features, filter_gains)
        return lax.dynamic_update_slice_in_dim(running, result, at, 0)

    group_total = (live_count + group_width - 1) // group_width
    return lax.fori_loop(0, group_total, block_advance, initial)


def join(features, places):
    padded = jnp.pad(places, ((0, 0), (0, 16 - places.shape[1]), (0, 0)))
    return jnp.concatenate([features, padded], axis=1)


def per_device(
    atom_features, positions, neighbours, counts, filter_gains, w_update, projections, w_output
):
    cells = lax.axis_size("cell")
    cell_index = lax.axis_index("cell")
    dirs_count = lax.axis_size("dir")
    dir_index = lax.axis_index("dir")
    capacity, block_atoms, width = atom_features.shape
    balanced_blocks = capacity // 2
    face_blocks = H
    faces = join(atom_features[:face_blocks], positions[:face_blocks])
    before = lax.ppermute(faces, "cell", [(i, (i + 1) % cells) for i in range(cells)])
    after = lax.ppermute(faces, "cell", [((i + 1) % cells, i) for i in range(cells)])
    float_positions = positions.astype(jnp.float32)
    extended_features = jnp.concatenate(
        [before[:, :block_atoms], atom_features, after[:, :block_atoms]], axis=0
    )
    axes = positions.shape[1]
    places_of = slice(block_atoms, block_atoms + axes)
    extended_positions = jnp.concatenate(
        [
            shift_component(before[:, places_of].astype(jnp.float32), -slab_width),
            float_positions,
            shift_component(after[:, places_of].astype(jnp.float32), slab_width),
        ],
        axis=0,
    )
    cell_order = jnp.arange(cells, dtype=jnp.int32)
    own_count = jnp.sum(jnp.where(cell_order == cell_index, counts, 0))
    first_live = jnp.sum(jnp.where(cell_order < cell_index, counts, 0))
    count_ends = jnp.cumsum(counts)
    share_slots = capacity // dirs_count
    first_slot = (dir_index - first_live) % dirs_count

    def mine(array):
        dealt = array.reshape((share_slots, dirs_count) + array.shape[1:])
        return lax.dynamic_index_in_dim(dealt, first_slot, 1, keepdims=False)

    live_count = (own_count - first_slot + dirs_count - 1) // dirs_count
    own_features = mine(atom_features)
    own_places = mine(positions)
    own_float = own_places.astype(jnp.float32)
    message = block_messages(
        live_count, 2, mine(neighbours), own_float, extended_features, extended_positions, filter_gains
    )
    activated = jax.nn.silu(message).astype(jnp.bfloat16)
    updated = (
        own_features.astype(jnp.float32)
        + jnp.dot(activated, w_update, preferred_element_type=jnp.float32)
    ).astype(jnp.bfloat16)

    share = DIRS // dirs_count
    unit_rows = 16 * cells
    padded_rows = -(-share * width // unit_rows) * unit_rows
    tables = jnp.asarray(direction_rows(DIRS, dirs_count))
    weights_t = projections.T
    own_global = shift_component(own_float, slab_width * cell_index.astype(jnp.float32))
    own_coords = jnp.transpose(own_global, (1, 0, 2)).reshape(axes, -1)
    live_atoms = (live_count * block_atoms).astype(jnp.int32).reshape(1)

    def states_of(owner, dtype):
        part = lax.dynamic_index_in_dim(tables, owner, 0, keepdims=False)
        return kv_states(
            live_atoms, part, own_coords, updated.reshape(-1, width), weights_t, projections, share,
            padded_rows, dtype,
        )

    away_states = states_of((dir_index + 1) % dirs_count, jnp.bfloat16)
    local_states = states_of(dir_index, jnp.float32)
    states = reduce_states(local_states, away_states, cells)

    slot_cap = max(1, 2 * balanced_blocks // cells)
    period = cells * slot_cap
    owner = jnp.arange(cells, dtype=jnp.int32)
    whole_rounds = slot_cap % dirs_count == 0
    per_owner = slot_cap // dirs_count if whole_rounds else slot_cap
    lane = jnp.arange(per_owner, dtype=jnp.int32)
    if whole_rounds:
        wanted = owner[:, None] * slot_cap + lane[None, :] * dirs_count + dir_index
    else:
        wanted = owner[:, None] * slot_cap + lane[None, :]
    offset = ((wanted - first_live) % period).reshape(-1)
    index = (offset - first_slot) // dirs_count
    is_mine = (offset < own_count) & ((offset - first_slot) % dirs_count == 0)
    picked = jnp.where(is_mine, index, 0)
    parcels = jnp.where(
        is_mine[:, None, None], join(updated, own_places)[picked], jnp.zeros((), jnp.bfloat16)
    )
    received = lax.all_to_all(parcels, "cell", split_axis=0, concat_axis=0, tiled=True)
    target = jnp.arange(balanced_blocks, dtype=jnp.int32)
    global_index = (target // slot_cap * cells + cell_index) * slot_cap + target % slot_cap
    source = jnp.sum((count_ends[None, :] <= global_index[:, None]).astype(jnp.int32), axis=1)
    if whole_rounds:
        def dealt_to(array, part):
            split = array.reshape((-1, dirs_count) + array.shape[1:])
            return lax.dynamic_index_in_dim(split, part, 1, keepdims=False)

        within = dealt_to(target % slot_cap, dir_index) // dirs_count
        rows = received[dealt_to(source, dir_index) * per_owner + within]
        gathered = [rows]
        for hop in range(1, dirs_count):
            gathered.append(
                lax.ppermute(rows, "dir", [(i, (i + hop) % dirs_count) for i in range(dirs_count)])
            )
        parts = jnp.stack(gathered, axis=1)
        order = (dir_index - jnp.arange(dirs_count, dtype=jnp.int32)) % dirs_count
        balanced = parts[:, order].reshape((balanced_blocks,) + parts.shape[2:])
    else:
        rows = received[source * per_owner + target % slot_cap]
        balanced = rows
        for hop in range(1, dirs_count):
            other = lax.ppermute(rows, "dir", [(i, (i + hop) % dirs_count) for i in range(dirs_count)])
            held = global_index % dirs_count == (dir_index - hop) % dirs_count
            balanced = jnp.where(held[:, None, None], other, balanced)
    balanced_features = balanced[:, :block_atoms]
    balanced_positions = shift_component(
        balanced[:, places_of].astype(jnp.float32),
        slab_width * source.astype(jnp.float32)[:, None, None],
    )
    share_blocks = balanced_blocks // dirs_count
    table = lax.dynamic_index_in_dim(tables, dir_index, 0, keepdims=False)

    def partial_mix(owner):
        features = lax.dynamic_slice_in_dim(balanced_features, owner * share_blocks, share_blocks, 0)
        places = lax.dynamic_slice_in_dim(balanced_positions, owner * share_blocks, share_blocks, 0)
        coords = jnp.transpose(places, (1, 0, 2)).reshape(axes, -1)
        return query_mix(table, coords, features.reshape(-1, width), weights_t, states, share)

    mixed_rows = None
    for hop in range(1, dirs_count):
        away = partial_mix((dir_index + hop) % dirs_count).astype(jnp.bfloat16)
        arrived = lax.ppermute(away, "dir", [(i, (i + hop) % dirs_count) for i in range(dirs_count)])
        arrived = arrived.astype(jnp.float32)
        mixed_rows = arrived if mixed_rows is None else mixed_rows + arrived
    kept = partial_mix(dir_index)
    mixed_rows = kept if mixed_rows is None else kept + mixed_rows
    mix_scale = 1.0 / math.sqrt(DIRS * cells * balanced_blocks * block_atoms * width)
    mixed = (mixed_rows * mix_scale).astype(jnp.bfloat16)
    attended = jnp.dot(mixed, w_output, preferred_element_type=jnp.float32).astype(jnp.bfloat16)
    return attended.reshape(-1, block_atoms, width)


def solution(mesh):
    placed = (
        P("cell", None, None),
        P("cell", None, None),
        P("cell", None),
        P(),
        P(),
        P(),
        P(),
        P(),
    )
    return jax.shard_map(
        per_device,
        mesh=mesh,
        in_specs=placed,
        out_specs=P(("cell", "dir"), None, None),
        check_vma=False,
    )
```

profile of v0, /device:TPU:0, one launch (start us, length us, event | category | flops | bytes accessed | tf_op | source)
XLA Modules:
  0.0 129.5 jit_solution(5418381298318806212)
XLA Ops:
  0.0 1.0 slice.24
  1.0 0.1 copy.55
  1.1 0.7 slice.25
  1.9 5.5 %collective-permute-start.1 = (bf16[4,144,128]{2,0,1:T(4,128)(2,1)S(1)}, bf16[4,144,128]{2,0,1:T(4,128)(2,1)S(1)}, u32[]{:S(2)}, u32[]{:S(2)}) collective-permute-start(bf16[4,144,128]{2,0,1:T(4,128)(2,1)S(1)} %fusion.20), channel_id=1, source_target_pairs={{2,0},{4,2},{6,4},{8,6},{10,8},{12,10},{14,12},{16,14},{18,16},{20... | collective-permute-start | bytes 442376 | tf_op jit(solution)/shard_map/ppermute | solution.py:404
  7.4 1.4 %fusion.32 = (s32[]{:T(128)}, s32[]{:T(128)}, s32[16]{0:T(128)S(1)}) fusion(s32[16]{0:T(128)} %param.14, s32[]{:T(128)S(6)} %axis_index.25), kind=kLoop, calls=%fused_computation.102 | loop fusion | flops 350 | bytes 140 | tf_op jit(solution)/shard_map/reduce_sum | solution.py:420
  9.4 0.7 copy.47
  10.2 0.1 reduce
  10.3 0.2 convert_reduce_fusion
  10.6 0.8 copy.40
  11.4 0.8 constant_dynamic-slice_fusion.4
  12.2 1.3 fusion.37
  13.5 0.2 fusion.25
  13.7 0.7 add_bitcast_fusion
  14.4 1.3 compare_and_fusion
  16.4 0.7 convert_element_type.79
  17.2 1.6 %copy.49 = bf16[128,384]{0,1:T(8,128)(2,1)} copy(bf16[128,384]{1,0:T(8,128)(2,1)} %weights_ref.3) | data formatting | bytes 196608 | tf_op args[6]
  18.8 0.6 dynamic-slice_bitcast_fusion.1
  19.8 0.2 pad_maximum_fusion
  20.0 1.1 broadcast_in_dim.27
  21.1 13.8 %while.10 = (s32[]{:T(128)}, f32[16,128,128]{2,1,0:T(8,128)}, s32[]{:T(128)}, f32[16,3,128]{2,1,0:T(4,128)S(1)}, s32[16,4]{1,0:T(8,128)S(1)}, /*index=5*/f32[40,...) while((s32[]{:T(128)}, f32[16,128,128]{2,1,0:T(8,128)}, ...), condition=%wide.region_5.6_spmd, body=%wide.region_2.0_spmd.sunk | while | flops 275219488 | bytes 3331535 | solution.py:384
  21.2 0.6 gather_fusion.1
  21.8 0.2 multiply_reduce_fusion.2
  22.0 0.1 sqrt.8
  22.2 0.6 gather_fusion
  22.8 1.1 fusion.52
  23.9 0.7 constant_dynamic-update-slice_fusion.2
  24.6 0.6 gather_fusion.1
  25.2 0.2 multiply_reduce_fusion.2
  25.5 0.1 sqrt.8
  25.6 0.6 gather_fusion
  26.2 1.1 fusion.52
  27.3 0.7 constant_dynamic-update-slice_fusion.2
  28.0 0.1 reshape.460
  28.1 0.6 gather_fusion.1
  28.7 0.2 multiply_reduce_fusion.2
  28.9 0.1 sqrt.8
  29.0 0.6 gather_fusion
  29.7 1.1 fusion.52
  30.8 0.7 constant_dynamic-update-slice_fusion.2
  31.5 0.6 gather_fusion.1
  32.1 0.2 multiply_reduce_fusion.2
  32.4 0.1 sqrt.8
  32.5 0.6 gather_fusion
  33.1 1.1 fusion.52
  34.2 0.7 constant_dynamic-update-slice_fusion.2
  34.9 1.6 %fusion.14 = bf16[16,128,128]{2,1,0:T(8,128)(2,1)S(1)} fusion(f32[16,128,128]{2,1,0:T(8,128)} %get-tuple-element.48, bf16[16,2,128,128]{3,2,1,0:T(8,128)(2,1)S(1)} %bitcast.74, s32[]{:T(128)S(6)} %select_n.199, bf16[128,128]{1,0:T(8,128)(2,1)S(1)} %copy-done), kind=kOutput, calls=%fused_computation.21 | convolution fusion | flops 69206016 | bytes 2129924 | tf_op jit(solution)/shard_map/dot_general | solution.py:440
  36.6 0.7 gather_fusion.2
  37.3 0.9 broadcast_select_fusion
  38.2 11.3 %all-to-all-start = ((bf16[16,144,128]{2,1,0:T(8,128)(2,1)}), bf16[16,144,128]{2,1,0:T(8,128)(2,1)S(1)}, u32[]{:S(2)}, u32[]{:S(2)}) async-start(bf16[16,144,128]{2,1,0:T(8,128)(2,1)} %broadcast_select_fusion), calls=%async_computation | async-start | bytes 1179648 | tf_op jit(solution)/shard_map/all_to_all | solution.py:480
  49.5 7.2 %kv_states.2.local_ref = f32[3328,128]{1,0:T(8,128)} custom-call(s32[1]{0:T(128)} %bitcast.25.live_ref, f32[32,128]{1,0:T(8,128)} %get-tuple-element.106.table_ref, f32[3,2048]{1,0:T(4,128)} %get-tuple-element.99.coords_ref, bf16[2048,128]{1,0:T(8,128)(2,1)} %bitcast.76, bf16[384,128]{1,0:T(8,128)(2,1)} %bitcast.82, bf16[128,384]{1,0:T(8,128)(2,1)} %weights_ref.3), custom_call_target="tpu_custom_call" | custom-call | flops 6710886400 | bytes 20000000 | tf_op jit(solution)/shard_map/kv_states/pallas_call | solution.py:170
  56.7 6.9 %kv_states.3.away_ref = bf16[3328,128]{1,0:T(8,128)(2,1)} custom-call(s32[1]{0:T(128)} %bitcast.25.live_ref, f32[32,128]{1,0:T(8,128)} %get-tuple-element.105.table_ref, f32[3,2048]{1,0:T(4,128)} %get-tuple-element.99.coords_ref, bf16[2048,128]{1,0:T(8,128)(2,1)} %bitcast.77, bf16[384,128]{1,0:T(8,128)(2,1)} %bitcast.83, bf16[128,384]{1,0:T(8,128)(2,1)} %weights_ref.3), custom_call_target="tpu_custom_call" | custom-call | flops 6710886400 | bytes 20000000 | tf_op jit(solution)/shard_map/kv_states/pallas_call | solution.py:170
  63.6 1.3 all-to-all-done
  64.9 0.6 gather_fusion.3
  65.5 1.6 %collective-permute-start.2 = (bf16[8,144,128]{2,1,0:T(8,128)(2,1)S(1)}, bf16[8,144,128]{2,1,0:T(8,128)(2,1)S(1)}, u32[]{:S(2)}, u32[]{:S(2)}) collective-permute-start(bf16[8,144,128]{2,1,0:T(8,128)(2,1)S(1)} %gather_fusion.3), channel_id=1, source_target_pairs={{0,1},{1,0},{2,3},{3,2},{4,5},{5,4},{6,7},{7,6},{8,9},{9,8},{10,11... | collective-permute-start | bytes 884744 | tf_op jit(solution)/shard_map/ppermute | solution.py:494
  67.1 41.1 %reduce_states.1.states_ref = bf16[3328,128]{1,0:T(8,128)(2,1)} custom-call(f32[3328,128]{1,0:T(8,128)} %kv_states.2.local_ref, bf16[3328,128]{1,0:T(8,128)(2,1)} %kv_states.3.away_ref), custom_call_target="tpu_custom_call" | custom-call | flops 20000000000 | bytes 60000000 | tf_op jit(solution)/shard_map/reduce_states/pallas_call | solution.py:339
  108.3 0.7 gather_fusion.4
  109.2 0.8 constant_dynamic-slice_fusion.1
  110.0 0.6 dynamic-slice_bitcast_fusion
  110.6 7.2 %query_mix.3 = f32[1024,128]{1,0:T(8,128)} custom-call(f32[32,128]{1,0:T(8,128)} %get-tuple-element.106.table_ref, f32[3,1024]{1,0:T(4,128)} %get-tuple-element.103.coords_ref, bf16[1024,128]{1,0:T(8,128)(2,1)} %bitcast.80, bf16[384,128]{1,0:T(8,128)(2,1)} %bitcast.84, bf16[3328,128]{1,0:T(8,128)(2,1)} %reduce_states.1.states_ref), custom_call_target="tpu_custom_call" | custom-call | flops 6710886400 | bytes 20000000 | tf_op jit(solution)/shard_map/query_mix/pallas_call | solution.py:192
  117.8 1.1 convert_element_type.88
  118.8 1.2 collective-permute-start.3
  120.1 7.2 %query_mix.2 = f32[1024,128]{1,0:T(8,128)} custom-call(f32[32,128]{1,0:T(8,128)} %get-tuple-element.106.table_ref, f32[3,1024]{1,0:T(4,128)} %get-tuple-element.104.coords_ref, bf16[1024,128]{1,0:T(8,128)(2,1)} %bitcast.79, bf16[384,128]{1,0:T(8,128)(2,1)} %bitcast.85, bf16[3328,128]{1,0:T(8,128)(2,1)} %reduce_states.1.states_ref), custom_call_target="tpu_custom_call" | custom-call | flops 6710886400 | bytes 20000000 | tf_op jit(solution)/shard_map/query_mix/pallas_call | solution.py:192
  127.2 0.3 collective-permute-done.3
  127.5 2.0 %convolution_convert_fusion = bf16[1024,128]{1,0:T(8,128)(2,1)} fusion(bf16[128,128]{1,0:T(8,128)(2,1)S(1)} %copy-done.3, f32[1024,128]{1,0:T(8,128)} %query_mix.2, bf16[1024,128]{1,0:T(8,128)(2,1)S(1)} %collective-permute-done.3), kind=kOutput, calls=%fused_computation.22 | convolution fusion | flops 34209792 | bytes 1081344 | tf_op jit(solution)/shard_map/dot_general | solution.py:530
  (63 shorter events, 1.3 us)
Async XLA Ops:
  0.0 34.9 %copy-start = (bf16[128,128]{1,0:T(8,128)(2,1)S(1)}, bf16[128,128]{1,0:T(8,128)(2,1)}, u32[]{:S(2)}) copy-start(bf16[128,128]{1,0:T(8,128)(2,1)} %param.16) | copy-start | bytes 98308
  0.0 18.8 %copy-start.4 = (f32[2,32,128]{2,1,0:T(8,128)S(1)}, f32[2,32,128]{2,1,0:T(8,128)}, u32[]{:S(2)}) copy-start(f32[2,32,128]{2,1,0:T(8,128)} %constant.207.clone) | copy-start | bytes 98308
  0.0 19.8 %copy-start.1 = (bf16[32,128,128]{2,1,0:T(8,128)(2,1)S(1)}, bf16[32,128,128]{2,1,0:T(8,128)(2,1)}, u32[]{:S(2)}) copy-start(bf16[32,128,128]{2,1,0:T(8,128)(2,1)} %param.11) | copy-start | bytes 3145732
  1.9 17.6 %collective-permute-start.1 = (bf16[4,144,128]{2,0,1:T(4,128)(2,1)S(1)}, bf16[4,144,128]{2,0,1:T(4,128)(2,1)S(1)}, u32[]{:S(2)}, u32[]{:S(2)}) collective-permute-start(bf16[4,144,128]{2,0,1:T(4,128)(2,1)S(1)} %fusion.20), channel_id=1, source_target_pairs={{2,0},{4,2},{6,4},{8,6},{10,8},{12,10},{14,12},{16,14},{18,16},{20... | collective-permute-start | bytes 442376 | tf_op jit(solution)/shard_map/ppermute | solution.py:404
  7.4 12.1 %collective-permute-start = (bf16[4,144,128]{2,0,1:T(4,128)(2,1)S(1)}, bf16[4,144,128]{2,0,1:T(4,128)(2,1)S(1)}, u32[]{:S(2)}, u32[]{:S(2)}) collective-permute-start(bf16[4,144,128]{2,0,1:T(4,128)(2,1)S(1)} %fusion.20), channel_id=1, source_target_pairs={{0,2},{2,4},{4,6},{6,8},{8,10},{10,12},{12,14},{14,16},{16,18},{18... | collective-permute-start | bytes 442376 | tf_op jit(solution)/shard_map/ppermute | solution.py:403
  19.8 1.3 copy-start.5
  36.5 1.7 %copy-start.2 = (bf16[16,128,128]{2,1,0:T(8,128)(2,1)}, bf16[16,128,128]{2,1,0:T(8,128)(2,1)S(1)}, u32[]{:S(2)}) copy-start(bf16[16,128,128]{2,1,0:T(8,128)(2,1)S(1)} %fusion.14) | copy-start | bytes 1572868
  38.2 26.7 %all-to-all-start = ((bf16[16,144,128]{2,1,0:T(8,128)(2,1)}), bf16[16,144,128]{2,1,0:T(8,128)(2,1)S(1)}, u32[]{:S(2)}, u32[]{:S(2)}) async-start(bf16[16,144,128]{2,1,0:T(8,128)(2,1)} %broadcast_select_fusion), calls=%async_computation | async-start | bytes 1179648 | tf_op jit(solution)/shard_map/all_to_all | solution.py:480
  65.5 42.7 %collective-permute-start.2 = (bf16[8,144,128]{2,1,0:T(8,128)(2,1)S(1)}, bf16[8,144,128]{2,1,0:T(8,128)(2,1)S(1)}, u32[]{:S(2)}, u32[]{:S(2)}) collective-permute-start(bf16[8,144,128]{2,1,0:T(8,128)(2,1)S(1)} %gather_fusion.3), channel_id=1, source_target_pairs={{0,1},{1,0},{2,3},{3,2},{4,5},{5,4},{6,7},{7,6},{8,9},{9,8},{10,11... | collective-permute-start | bytes 884744 | tf_op jit(solution)/shard_map/ppermute | solution.py:494
  118.8 8.7 %collective-permute-start.3 = (bf16[1024,128]{1,0:T(8,128)(2,1)S(1)}, bf16[1024,128]{1,0:T(8,128)(2,1)S(1)}, u32[]{:S(2)}, u32[]{:S(2)}) collective-permute-start(bf16[1024,128]{1,0:T(8,128)(2,1)S(1)} %convert_element_type.88), channel_id=1, source_target_pairs={{0,1},{1,0},{2,3},{3,2},{4,5},{5,4},{6,7},{7,6},{8,9},{9,8},{10,11... | collective-permute-start | bytes 786440 | tf_op jit(solution)/shard_map/ppermute | solution.py:523
  120.1 7.5 %copy-start.3 = (bf16[128,128]{1,0:T(8,128)(2,1)S(1)}, bf16[128,128]{1,0:T(8,128)(2,1)}, u32[]{:S(2)}) copy-start(bf16[128,128]{1,0:T(8,128)(2,1)} %param.18) | copy-start | bytes 98308
where the time goes:
time: 131 us; the launch traced here: 129 us
  Pallas kernels  69.5 us (53%)
  starting transfers between devices  19.6 us (15%)
  local copies, waits for them, and re-layouts  19.4 us (15%)
  other arithmetic  9.53 us (7%)
  matrix products  8.06 us (6%)
  waiting for transfers between devices  1.59 us (1%)
  between operations  1.59 us (1%)
    pallas_call x1, Pallas kernels, reduce_states(): pl.pallas_call(functools.partial(reduce_kernel, bits), out_shape=jax.Shap...  41.1 us
    pallas_call x2, Pallas kernels, query_mix(): pl.pallas_call(functools.partial(query_kernel, chunk, share), out_shape=j...  14.3 us
    pallas_call x2, Pallas kernels, kv_states(): pl.pallas_call(functools.partial(kv_kernel, chunk, share), out_shape=jax....  14.1 us
    all_to_all x1, starting transfers between devices, per_device(): lax.all_to_all(parcels, 'cell', split_axis=0, concat_axis=0, tiled=True)  11.3 us
    ppermute x1, starting transfers between devices, per_device(): lax.ppermute(faces, 'cell', [((i + 1) % cells, i) for i in range(cells)])  5.53 us
    dot_general x4, matrix products, radial_terms(): jnp.einsum('gnkab,gnbf->gkaf', radial, near_features, preferred_element_t...  4.45 us
    dynamic_update_slice x4, local copies, waits for them, and re-layouts, block_advance(): return lax.dynamic_update_slice_in_dim(running, result, at, 0)  2.66 us
  transfers between devices with their start and end apart: 5, of which 2 were waited for; matrix products, arithmetic and copies ran while one was open for 8% of the time, Pallas kernels for 48%

commit v1 on v0

--- a/solution.py
+++ b/solution.py
@@ -15,6 +15,7 @@
 
 slab_width = 12.0
 radial_width = 0.6
+radial_scale = math.sqrt(math.log2(math.e)) / radial_width
 golden_turn = math.pi * (3.0 - math.sqrt(5.0))
 
 
@@ -166,7 +167,7 @@
     width = flat.shape[1]
     chunk = 256
     count = table.shape[0]
-    atoms = flat.shape[0] // 2
+    atoms = flat.shape[0]
     return pl.pallas_call(
         functools.partial(kv_kernel, chunk, share),
         out_shape=jax.ShapeDtypeStruct((padded_rows, width), dtype),
@@ -353,40 +354,177 @@
     )(local, away)
 
 
-def radial_terms(own_positions, near_positions, near_features, filter_gains):
-    differ = own_positions[:, None, :, :, None] - near_positions[:, :, :, None, :]
-    distance = jnp.sqrt(jnp.sum(differ * differ, axis=2))
-    centers = 2.0 + 2.0 * jnp.arange(filter_gains.shape[0], dtype=jnp.float32)
-    scaled = (distance[:, :, None] - centers[None, None, :, None, None]) / radial_width
-    radial = jnp.exp(-scaled * scaled).astype(jnp.bfloat16)
-    summed = jnp.einsum(
-        "gnkab,gnbf->gkaf", radial, near_features, preferred_element_type=jnp.float32
-    )
-    return jnp.sum(summed * filter_gains[None, :, None, :], axis=1)
-
-
-def block_messages(live_count, group_width, picks, own_positions, extended_features, extended_positions, filter_gains):
-    slot_count = picks.shape[0]
-    initial = jnp.zeros(
-        (slot_count, extended_features.shape[1], extended_features.shape[2]), jnp.float32
-    )
-
-    def block_advance(turn_index, running):
-        at = turn_index * group_width
-        picked = lax.dynamic_slice_in_dim(picks, at, group_width, 0)
-        near_features = extended_features[picked]
-        near_positions = extended_positions[picked]
-        own = lax.dynamic_slice_in_dim(own_positions, at, group_width, 0)
-        result = radial_terms(own, near_positions, near_features, filter_gains)
-        return lax.dynamic_update_slice_in_dim(running, result, at, 0)
-
-    group_total = (live_count + group_width - 1) // group_width
-    return lax.fori_loop(0, group_total, block_advance, initial)
-
-
-def join(features, places):
-    padded = jnp.pad(places, ((0, 0), (0, 16 - places.shape[1]), (0, 0)))
-    return jnp.concatenate([features, padded], axis=1)
+def bits_of(count):
+    return count.bit_length() - 1
+
+
+def message_kernel(
+    cells, dirs, slot_cap, per_owner, entries_ref, counts_ref, places_ref, gains_ref, update_ref, features_ref,
+    received_ref, near, raw, scaled, face_out, face_in, parcels, local_sem, face_send, face_recv, send_sems, recv_sems,
+):
+    me = lax.axis_index("cell")
+    turn = lax.axis_index("dir")
+    capacity = features_ref.shape[0]
+    block, width = features_ref.shape[1], features_ref.shape[2]
+    faces = H
+    before, after = lax.rem(me + cells - 1, cells), lax.rem(me + 1, cells)
+    own_copy = pltpu.make_async_copy(features_ref, near.at[pl.ds(0, capacity)], local_sem)
+    own_copy.start()
+    barrier = pltpu.get_barrier_semaphore()
+
+    def greet(k, carried):
+        pl.semaphore_signal(
+            barrier, inc=1, device_id={"cell": lax.rem(me + k, cells)}, device_id_type=pl.DeviceIdType.MESH
+        )
+        return carried
+
+    lax.fori_loop(1, cells, greet, 0)
+    axes = places_ref.shape[0]
+    for axis in range(axes):
+        lifted = places_ref[axis].astype(jnp.float32)
+        raw[axis, 0:capacity, :] = lifted
+        scaled[axis, 0:capacity, :] = lifted * radial_scale
+        face_out[axis * faces : (axis + 1) * faces, :] = lifted[0:faces]
+    pl.semaphore_wait(barrier, cells - 1)
+
+    face_copies = []
+    for side, device in ((0, after), (1, before)):
+        landing = pl.ds(capacity + side * faces, faces)
+        pairs = (
+            (features_ref.at[pl.ds(0, faces)], near.at[landing]),
+            (face_out, face_in.at[side]),
+        )
+        for kind, (source, target) in enumerate(pairs):
+            copy = pltpu.make_async_remote_copy(
+                src_ref=source, dst_ref=target, send_sem=face_send.at[side, kind],
+                recv_sem=face_recv.at[side, kind], device_id={"cell": device},
+                device_id_type=pl.DeviceIdType.MESH,
+            )
+            copy.start()
+            face_copies.append(copy)
+
+    first_live = lax.fori_loop(0, me, lambda c, total: total + counts_ref[c], jnp.int32(0))
+    own_count = counts_ref[me]
+    first_slot = lax.rem(turn + dirs * cells * capacity - first_live, dirs)
+    period = cells * slot_cap
+    own_copy.wait()
+    for copy in face_copies:
+        copy.wait_recv()
+    for side, shift in ((0, -slab_width), (1, slab_width)):
+        for axis in range(axes):
+            moved = face_in[side, axis * faces : (axis + 1) * faces, :]
+            if axis == 0:
+                moved = moved + shift
+            scaled[axis, capacity + side * faces : capacity + (side + 1) * faces, :] = moved * radial_scale
+
+    centers = [(2.0 + 2.0 * k) * radial_scale for k in range(gains_ref.shape[0])]
+    row = lax.broadcasted_iota(jnp.int32, (16, width), 0)
+
+    def serve(step, carried):
+        item = step
+        destination = lax.rem(me + 1 + step // per_owner, cells)
+        lane = lax.rem(step, per_owner)
+        if per_owner * dirs == slot_cap:
+            wanted = destination * slot_cap + lane * dirs + turn
+        else:
+            wanted = destination * slot_cap + lane
+        offset = lax.rem(wanted + period * capacity * cells - first_live, period)
+        mine = (offset < own_count) & (lax.rem(offset + dirs - first_slot, dirs) == 0)
+        slot = jnp.where(mine, offset, 0)
+        columns = []
+        for axis in range(axes):
+            line = jnp.broadcast_to(scaled[axis, pl.ds(slot, 1), :], (block, block))
+            columns.append(line.T)
+        features, distances = [], []
+        for j in range(entries_ref.shape[0]):
+            entry = entries_ref[j, slot]
+            place = jnp.where(entry < faces, capacity + entry, jnp.where(entry < faces + capacity, entry - faces, entry))
+            features.append(near[place])
+            square = None
+            for axis in range(axes):
+                differ = columns[axis] - scaled[axis, pl.ds(place, 1), :]
+                term = differ * differ
+                square = term if square is None else square + term
+            distances.append(jnp.sqrt(square))
+        message = None
+        stacked = jnp.concatenate(features, axis=0)
+        for k, center in enumerate(centers):
+            parts = []
+            for distance in distances:
+                away = distance - center
+                parts.append(jnp.exp2(-(away * away)).astype(jnp.bfloat16))
+            summed = jnp.dot(jnp.concatenate(parts, axis=1), stacked, preferred_element_type=jnp.float32)
+            summed = summed * gains_ref[k : k + 1, :]
+            message = summed if message is None else message + summed
+        activated = (message / (1.0 + jnp.exp(-message))).astype(jnp.bfloat16)
+        updated = near[slot].astype(jnp.float32) + jnp.dot(
+            activated, update_ref[...], preferred_element_type=jnp.float32
+        )
+        parcels[item, 0:block, :] = updated.astype(jnp.bfloat16)
+        held = jnp.zeros((16, width), jnp.float32)
+        for axis in range(axes):
+            held = jnp.where(row == axis, raw[axis, pl.ds(slot, 1), :], held)
+        parcels[item, block : block + 16, :] = held.astype(jnp.bfloat16)
+
+        @pl.when(step < (cells - 1) * per_owner)
+        def _():
+            pltpu.make_async_remote_copy(
+                src_ref=parcels.at[item], dst_ref=received_ref.at[me * per_owner + lane],
+                send_sem=send_sems.at[step], recv_sem=recv_sems.at[step],
+                device_id={"cell": destination}, device_id_type=pl.DeviceIdType.MESH,
+            ).start()
+
+        return carried
+
+    lax.fori_loop(0, cells * per_owner, serve, 0)
+    for lane in range(per_owner):
+        received_ref[me * per_owner + lane] = parcels[(cells - 1) * per_owner + lane]
+    for copy in face_copies:
+        copy.wait_send()
+
+    def settle(step, carried):
+        lane = lax.rem(step, per_owner)
+        source = lax.rem(me + cells - 1 - step // per_owner, cells)
+        copy = pltpu.make_async_remote_copy(
+            src_ref=parcels.at[step], dst_ref=received_ref.at[source * per_owner + lane],
+            send_sem=send_sems.at[step], recv_sem=recv_sems.at[step],
+            device_id={"cell": lax.rem(me + 1 + step // per_owner, cells)},
+            device_id_type=pl.DeviceIdType.MESH,
+        )
+        copy.wait_recv()
+        copy.wait_send()
+        return carried
+
+    lax.fori_loop(0, (cells - 1) * per_owner, settle, 0)
+
+
+def deal_updates(entries, counts, places, gains, w_update, features, cells, dirs, slot_cap, per_owner):
+    capacity, block, width = features.shape
+    axes = places.shape[0]
+    total = capacity + 2 * H
+    items = cells * per_owner
+    return pl.pallas_call(
+        functools.partial(message_kernel, cells, dirs, slot_cap, per_owner),
+        out_shape=jax.ShapeDtypeStruct((items, block + 16, width), jnp.bfloat16),
+        in_specs=[pl.BlockSpec(memory_space=pltpu.SMEM)] * 2 + vmem(3) + [pl.BlockSpec(memory_space=pl.ANY)],
+        out_specs=pl.BlockSpec(memory_space=pltpu.VMEM),
+        scratch_shapes=[
+            pltpu.VMEM((total, block, width), jnp.bfloat16),
+            pltpu.VMEM((axes, capacity, width), jnp.float32),
+            pltpu.VMEM((axes, total, width), jnp.float32),
+            pltpu.VMEM((axes * H, width), jnp.float32),
+            pltpu.VMEM((2, axes * H, width), jnp.float32),
+            pltpu.VMEM((items, block + 16, width), jnp.bfloat16),
+            pltpu.SemaphoreType.DMA,
+            pltpu.SemaphoreType.DMA((2, 2)),
+            pltpu.SemaphoreType.DMA((2, 2)),
+            pltpu.SemaphoreType.DMA((items,)),
+            pltpu.SemaphoreType.DMA((items,)),
+        ],
+        compiler_params=pltpu.CompilerParams(collective_id=1, has_side_effects=True),
+        cost_estimate=pl.CostEstimate(flops=20_000_000_000, bytes_accessed=4_000_000, transcendentals=0),
+        name="deal_updates",
+    )(entries, counts, places, gains, w_update, features)
 
 
 def per_device(
@@ -398,86 +536,22 @@
     dir_index = lax.axis_index("dir")
     capacity, block_atoms, width = atom_features.shape
     balanced_blocks = capacity // 2
-    face_blocks = H
-    faces = join(atom_features[:face_blocks], positions[:face_blocks])
-    before = lax.ppermute(faces, "cell", [(i, (i + 1) % cells) for i in range(cells)])
-    after = lax.ppermute(faces, "cell", [((i + 1) % cells, i) for i in range(cells)])
-    float_positions = positions.astype(jnp.float32)
-    extended_features = jnp.concatenate(
-        [before[:, :block_atoms], atom_features, after[:, :block_atoms]], axis=0
-    )
     axes = positions.shape[1]
     places_of = slice(block_atoms, block_atoms + axes)
-    extended_positions = jnp.concatenate(
-        [
-            shift_component(before[:, places_of].astype(jnp.float32), -slab_width),
-            float_positions,
-            shift_component(after[:, places_of].astype(jnp.float32), slab_width),
-        ],
-        axis=0,
-    )
-    cell_order = jnp.arange(cells, dtype=jnp.int32)
-    own_count = jnp.sum(jnp.where(cell_order == cell_index, counts, 0))
-    first_live = jnp.sum(jnp.where(cell_order < cell_index, counts, 0))
     count_ends = jnp.cumsum(counts)
-    share_slots = capacity // dirs_count
-    first_slot = (dir_index - first_live) % dirs_count
-
-    def mine(array):
-        dealt = array.reshape((share_slots, dirs_count) + array.shape[1:])
-        return lax.dynamic_index_in_dim(dealt, first_slot, 1, keepdims=False)
-
-    live_count = (own_count - first_slot + dirs_count - 1) // dirs_count
-    own_features = mine(atom_features)
-    own_places = mine(positions)
-    own_float = own_places.astype(jnp.float32)
-    message = block_messages(
-        live_count, 2, mine(neighbours), own_float, extended_features, extended_positions, filter_gains
-    )
-    activated = jax.nn.silu(message).astype(jnp.bfloat16)
-    updated = (
-        own_features.astype(jnp.float32)
-        + jnp.dot(activated, w_update, preferred_element_type=jnp.float32)
-    ).astype(jnp.bfloat16)
 
     share = DIRS // dirs_count
     unit_rows = 16 * cells
     padded_rows = -(-share * width // unit_rows) * unit_rows
     tables = jnp.asarray(direction_rows(DIRS, dirs_count))
     weights_t = projections.T
-    own_global = shift_component(own_float, slab_width * cell_index.astype(jnp.float32))
-    own_coords = jnp.transpose(own_global, (1, 0, 2)).reshape(axes, -1)
-    live_atoms = (live_count * block_atoms).astype(jnp.int32).reshape(1)
-
-    def states_of(owner, dtype):
-        part = lax.dynamic_index_in_dim(tables, owner, 0, keepdims=False)
-        return kv_states(
-            live_atoms, part, own_coords, updated.reshape(-1, width), weights_t, projections, share,
-            padded_rows, dtype,
-        )
-
-    away_states = states_of((dir_index + 1) % dirs_count, jnp.bfloat16)
-    local_states = states_of(dir_index, jnp.float32)
-    states = reduce_states(local_states, away_states, cells)
-
     slot_cap = max(1, 2 * balanced_blocks // cells)
-    period = cells * slot_cap
-    owner = jnp.arange(cells, dtype=jnp.int32)
     whole_rounds = slot_cap % dirs_count == 0
     per_owner = slot_cap // dirs_count if whole_rounds else slot_cap
-    lane = jnp.arange(per_owner, dtype=jnp.int32)
-    if whole_rounds:
-        wanted = owner[:, None] * slot_cap + lane[None, :] * dirs_count + dir_index
-    else:
-        wanted = owner[:, None] * slot_cap + lane[None, :]
-    offset = ((wanted - first_live) % period).reshape(-1)
-    index = (offset - first_slot) // dirs_count
-    is_mine = (offset < own_count) & ((offset - first_slot) % dirs_count == 0)
-    picked = jnp.where(is_mine, index, 0)
-    parcels = jnp.where(
-        is_mine[:, None, None], join(updated, own_places)[picked], jnp.zeros((), jnp.bfloat16)
+    received = deal_updates(
+        neighbours.T, counts, jnp.transpose(positions, (1, 0, 2)), filter_gains, w_update, atom_features,
+        cells, dirs_count, slot_cap, per_owner,
     )
-    received = lax.all_to_all(parcels, "cell", split_axis=0, concat_axis=0, tiled=True)
     target = jnp.arange(balanced_blocks, dtype=jnp.int32)
     global_index = (target // slot_cap * cells + cell_index) * slot_cap + target % slot_cap
     source = jnp.sum((count_ends[None, :] <= global_index[:, None]).astype(jnp.int32), axis=1)
@@ -508,6 +582,36 @@
         balanced[:, places_of].astype(jnp.float32),
         slab_width * source.astype(jnp.float32)[:, None, None],
     )
+    def coords_of(places):
+        return jnp.transpose(places, (1, 0, 2)).reshape(axes, -1)
+
+    if whole_rounds:
+        kv_blocks = rows[:, :block_atoms]
+        kv_places = shift_component(
+            rows[:, places_of].astype(jnp.float32),
+            slab_width * dealt_to(source, dir_index).astype(jnp.float32)[:, None, None],
+        )
+    else:
+        kv_blocks, kv_places = [
+            lax.dynamic_slice_in_dim(
+                array, dir_index * (balanced_blocks // dirs_count), balanced_blocks // dirs_count, 0
+            )
+            for array in (balanced_features, balanced_positions)
+        ]
+    own_coords = coords_of(kv_places)
+    live_atoms = jnp.full((1,), own_coords.shape[1], jnp.int32)
+
+    def states_of(owner, dtype):
+        part = lax.dynamic_index_in_dim(tables, owner, 0, keepdims=False)
+        return kv_states(
+            live_atoms, part, own_coords, kv_blocks.reshape(-1, width), weights_t, projections, share,
+            padded_rows, dtype,
+        )
+
+    away_states = states_of((dir_index + 1) % dirs_count, jnp.bfloat16)
+    local_states = states_of(dir_index, jnp.float32)
+    states = reduce_states(local_states, away_states, cells)
+
     share_blocks = balanced_blocks // dirs_count
     table = lax.dynamic_index_in_dim(tables, dir_index, 0, keepdims=False)
 

time: 131 us -> 109 us (0.83); the launches traced: 129 us -> 109 us
  Pallas kernels: 69.5 us -> 94.1 us
  starting transfers between devices: 19.6 us -> 3.23 us
  local copies, waits for them, and re-layouts: 19.4 us -> 6.77 us
  other arithmetic: 9.53 us -> 2.79 us
  matrix products: 8.06 us -> 1.96 us
  waiting for transfers between devices: 1.59 us -> 0.01 us
  between operations: 1.59 us -> 0.14 us
    pallas_call x0 -> x1, Pallas kernels: none -> 27.9 us  [deal_updates(): pl.pallas_call(functools.partial(message_kernel, cells, dirs, slot_cap, p...]
    all_to_all x1 -> x0, starting transfers between devices: 11.3 us -> none  [per_device(): lax.all_to_all(parcels, 'cell', split_axis=0, concat_axis=0, tiled=True)]
    dot_general x5 -> x0, matrix products: 6.09 us -> none  [the longest x4 4.45 us: radial_terms(): jnp.einsum('gnkab,gnbf->gkaf', radial, near_features, preferred_element_t...]
    ppermute x2 -> x0, starting transfers between devices: 5.53 us -> none  [the longest x1 5.53 us: per_device(): lax.ppermute(faces, 'cell', [((i + 1) % cells, i) for i in range(cells)])]
    gather x9 -> x0, local copies, waits for them, and re-layouts: 5.34 us -> none  [the longest x4 2.39 us: block_advance(): near_features = extended_features[picked]]
    pallas_call x1, Pallas kernels: 41.1 us -> 38 us  [reduce_states(): pl.pallas_call(functools.partial(reduce_kernel, bits), out_shape=jax.Shap...]
    dynamic_update_slice x4 -> x0, local copies, waits for them, and re-layouts: 2.66 us -> none  [block_advance(): return lax.dynamic_update_slice_in_dim(running, result, at, 0)]
    select_n x6 -> x0, other arithmetic: 2.23 us -> none  [the longest x1 1.27 us: per_device(): join(updated, own_places)[picked]]
  transfers between devices with their start and end apart: 5 -> 2, of which waited for: 2 -> 0; matrix products, arithmetic and copies ran while one was open for 8% -> 3% of each run, Pallas kernels for 48% -> 54%
where the time goes in v1:
time: 109 us
  Pallas kernels  94.1 us (86%)
  local copies, waits for them, and re-layouts  6.77 us (6%)
  starting transfers between devices  3.23 us (3%)
  other arithmetic  2.79 us (3%)
  matrix products  1.96 us (2%)
    pallas_call x1, Pallas kernels, reduce_states(): pl.pallas_call(functools.partial(reduce_kernel, bits), out_shape=jax.Shap...  38 us
    pallas_call x1, Pallas kernels, deal_updates(): pl.pallas_call(functools.partial(message_kernel, cells, dirs, slot_cap, p...  27.9 us
    pallas_call x2, Pallas kernels, query_mix(): pl.pallas_call(functools.partial(query_kernel, chunk, share), out_shape=j...  14.3 us
    pallas_call x2, Pallas kernels, kv_states(): pl.pallas_call(functools.partial(kv_kernel, chunk, share), out_shape=jax....  13.9 us
  transfers between devices with their start and end apart: 2, of which 0 were waited for; matrix products, arithmetic and copies ran while one was open for 3% of the time, Pallas kernels for 54%

profile of v1, /device:TPU:0, one launch (start us, length us, event | category | flops | bytes accessed | tf_op | source)
XLA Modules:
  0.0 109.0 jit_solution(7043171431826843466)
XLA Ops:
  0.0 0.0 copy-start
  0.0 0.7 copy.15
  0.8 0.1 reduce
  0.9 0.2 convert_reduce_fusion
  1.1 0.1 reshape.214
  1.2 0.2 fusion.4
  1.4 0.0 copy-start.1
  1.4 0.0 copy-start.2
  1.4 27.9 %deal_updates.1 = bf16[16,144,128]{2,1,0:T(8,128)(2,1)} custom-call(s32[4,32]{1,0:T(4,128)} %bitcast.46, s32[16]{0:T(128)} %counts_ref.1, bf16[3,32,128]{2,1,0:T(8,128)(2,1)} %bitcast.45, f32[8,128]{1,0:T(8,128)} %gains_ref.1, bf16[128,128]{1,0:T(8,128)(2,1)} %update_ref.1, bf16[32,128,128]{2,1,0:T(8,128)(2,1)} %features_ref.1), custom_call_target="tpu_custom_call" | custom-call | flops 20000000000 | bytes 4000000 | tf_op jit(solution)/shard_map/deal_updates/pallas_call | solution.py:506
  29.3 1.7 %gather_fusion = bf16[8,144,128]{2,1,0:T(8,128)(2,1)S(1)} fusion(bf16[16,144,128]{2,1,0:T(8,128)(2,1)} %deal_updates.1, s32[1024]{0:T(1024)S(1)} %pad_clamp_fusion.1), kind=kCustom, calls=%fused_computation | custom fusion | bytes 589856 | tf_op jit(solution)/shard_map/gather | solution.py:564
  31.0 1.6 %collective-permute-start = (bf16[8,144,128]{2,1,0:T(8,128)(2,1)S(1)}, bf16[8,144,128]{2,1,0:T(8,128)(2,1)S(1)}, u32[]{:S(2)}, u32[]{:S(2)}) collective-permute-start(bf16[8,144,128]{2,1,0:T(8,128)(2,1)S(1)} %gather_fusion), channel_id=1, source_target_pairs={{0,1},{1,0},{2,3},{3,2},{4,5},{5,4},{6,7},{7,6},{8,9},{9,8},{10,11... | collective-permute-start | bytes 884744 | tf_op jit(solution)/shard_map/ppermute | solution.py:568
  32.6 0.2 multiply_reduce_fusion
  32.7 0.7 slice.23
  33.5 0.1 broadcast_multiply_fusion.1
  33.6 0.7 add_bitcast_fusion.coords_ref
  34.2 0.0 copy-done.1
  34.2 0.7 copy.17
  35.0 0.0 copy-done.2
  35.0 0.6 dynamic-slice_bitcast_fusion.1
  35.6 7.1 %kv_states.2.local_ref = f32[3328,128]{1,0:T(8,128)} custom-call(s32[1]{0:T(128)} %constant.107.clone.1.live_ref, f32[32,128]{1,0:T(8,128)} %get-tuple-element.10.table_ref, f32[3,1024]{1,0:T(4,128)} %add_bitcast_fusion.coords_ref, bf16[1024,128]{1,0:T(8,128)(2,1)} %bitcast.38, bf16[384,128]{1,0:T(8,128)(2,1)} %bitcast.40, bf16[128,384]{1,0:T(8,128)(2,1)} %weights_ref.3), custom_call_target="tpu_custom_call" | custom-call | flops 6710886400 | bytes 20000000 | tf_op jit(solution)/shard_map/kv_states/pallas_call | solution.py:171
  42.7 6.8 %kv_states.3.away_ref = bf16[3328,128]{1,0:T(8,128)(2,1)} custom-call(s32[1]{0:T(128)} %constant.107.clone.1.live_ref, f32[32,128]{1,0:T(8,128)} %get-tuple-element.9.table_ref, f32[3,1024]{1,0:T(4,128)} %add_bitcast_fusion.coords_ref, bf16[1024,128]{1,0:T(8,128)(2,1)} %bitcast.39, bf16[384,128]{1,0:T(8,128)(2,1)} %bitcast.41, bf16[128,384]{1,0:T(8,128)(2,1)} %weights_ref.3), custom_call_target="tpu_custom_call" | custom-call | flops 6710886400 | bytes 20000000 | tf_op jit(solution)/shard_map/kv_states/pallas_call | solution.py:171
  49.5 38.0 %reduce_states.1.states_ref = bf16[3328,128]{1,0:T(8,128)(2,1)} custom-call(f32[3328,128]{1,0:T(8,128)} %kv_states.2.local_ref, bf16[3328,128]{1,0:T(8,128)(2,1)} %kv_states.3.away_ref), custom_call_target="tpu_custom_call" | custom-call | flops 20000000000 | bytes 60000000 | tf_op jit(solution)/shard_map/reduce_states/pallas_call | solution.py:340
  87.5 0.1 broadcast_multiply_fusion
  87.6 0.0 collective-permute-done
  87.6 0.1 pad_maximum_fusion
  87.7 0.7 gather_fusion.1
  88.4 0.1 convert_add_fusion
  88.5 0.8 constant_dynamic-slice_fusion
  89.3 0.6 dynamic-slice_bitcast_fusion
  90.0 7.2 %query_mix.3 = f32[1024,128]{1,0:T(8,128)} custom-call(f32[32,128]{1,0:T(8,128)} %get-tuple-element.10.table_ref, f32[3,1024]{1,0:T(4,128)} %get-tuple-element.7.coords_ref, bf16[1024,128]{1,0:T(8,128)(2,1)} %bitcast.37, bf16[384,128]{1,0:T(8,128)(2,1)} %bitcast.42, bf16[3328,128]{1,0:T(8,128)(2,1)} %reduce_states.1.states_ref), custom_call_target="tpu_custom_call" | custom-call | flops 6710886400 | bytes 20000000 | tf_op jit(solution)/shard_map/query_mix/pallas_call | solution.py:193
  97.1 1.1 convert_element_type.52
  98.2 1.7 %collective-permute-start.1 = (bf16[1024,128]{1,0:T(8,128)(2,1)S(1)}, bf16[1024,128]{1,0:T(8,128)(2,1)S(1)}, u32[]{:S(2)}, u32[]{:S(2)}) collective-permute-start(bf16[1024,128]{1,0:T(8,128)(2,1)S(1)} %convert_element_type.52), channel_id=1, source_target_pairs={{0,1},{1,0},{2,3},{3,2},{4,5},{5,4},{6,7},{7,6},{8,9},{9,8},{10,11... | collective-permute-start | bytes 786440 | tf_op jit(solution)/shard_map/ppermute | solution.py:627
  99.9 7.2 %query_mix.2 = f32[1024,128]{1,0:T(8,128)} custom-call(f32[32,128]{1,0:T(8,128)} %get-tuple-element.10.table_ref, f32[3,1024]{1,0:T(4,128)} %get-tuple-element.8.coords_ref, bf16[1024,128]{1,0:T(8,128)(2,1)} %bitcast.36, bf16[384,128]{1,0:T(8,128)(2,1)} %bitcast.43, bf16[3328,128]{1,0:T(8,128)(2,1)} %reduce_states.1.states_ref), custom_call_target="tpu_custom_call" | custom-call | flops 6710886400 | bytes 20000000 | tf_op jit(solution)/shard_map/query_mix/pallas_call | solution.py:193
  107.0 0.0 collective-permute-done.1
  107.0 0.0 copy-done
  107.0 2.0 %convolution_convert_fusion = bf16[1024,128]{1,0:T(8,128)(2,1)} fusion(bf16[128,128]{1,0:T(8,128)(2,1)S(1)} %copy-done, f32[1024,128]{1,0:T(8,128)} %query_mix.2, bf16[1024,128]{1,0:T(8,128)(2,1)S(1)} %collective-permute-done.1), kind=kOutput, calls=%fused_computation.2 | convolution fusion | flops 34209792 | bytes 1081344 | tf_op jit(solution)/shard_map/dot_general | solution.py:634
  (10 shorter events, 0.2 us)
Async XLA Ops:
  0.0 107.0 %copy-start = (bf16[128,128]{1,0:T(8,128)(2,1)S(1)}, bf16[128,128]{1,0:T(8,128)(2,1)}, u32[]{:S(2)}) copy-start(bf16[128,128]{1,0:T(8,128)(2,1)} %param.16) | copy-start | bytes 98308
  1.4 32.8 %copy-start.1 = (bf16[128,384]{1,0:T(8,128)(2,1)S(1)}, bf16[128,384]{1,0:T(8,128)(2,1)}, u32[]{:S(2)}) copy-start(bf16[128,384]{1,0:T(8,128)(2,1)} %weights_ref.3) | copy-start | bytes 294916
  1.4 33.6 %copy-start.2 = (f32[2,32,128]{2,1,0:T(8,128)S(1)}, f32[2,32,128]{2,1,0:T(8,128)}, u32[]{:S(2)}) copy-start(f32[2,32,128]{2,1,0:T(8,128)} %constant.109.clone) | copy-start | bytes 98308
  31.0 56.6 %collective-permute-start = (bf16[8,144,128]{2,1,0:T(8,128)(2,1)S(1)}, bf16[8,144,128]{2,1,0:T(8,128)(2,1)S(1)}, u32[]{:S(2)}, u32[]{:S(2)}) collective-permute-start(bf16[8,144,128]{2,1,0:T(8,128)(2,1)S(1)} %gather_fusion), channel_id=1, source_target_pairs={{0,1},{1,0},{2,3},{3,2},{4,5},{5,4},{6,7},{7,6},{8,9},{9,8},{10,11... | collective-permute-start | bytes 884744 | tf_op jit(solution)/shard_map/ppermute | solution.py:568
  98.2 8.8 %collective-permute-start.1 = (bf16[1024,128]{1,0:T(8,128)(2,1)S(1)}, bf16[1024,128]{1,0:T(8,128)(2,1)S(1)}, u32[]{:S(2)}, u32[]{:S(2)}) collective-permute-start(bf16[1024,128]{1,0:T(8,128)(2,1)S(1)} %convert_element_type.52), channel_id=1, source_target_pairs={{0,1},{1,0},{2,3},{3,2},{4,5},{5,4},{6,7},{7,6},{8,9},{9,8},{10,11... | collective-permute-start | bytes 786440 | tf_op jit(solution)/shard_map/ppermute | solution.py:627

commit v2 on v1

v2 whole, which is shorter than its diff:
```python
import functools
import math

import jax
import jax.numpy as jnp
import numpy as np
from jax import lax
from jax.experimental import pallas as pl
from jax.experimental.pallas import tpu as pltpu
from jax.sharding import PartitionSpec as P

DIRS = 50
H = 4


slab_width = 12.0
radial_width = 0.6
radial_scale = math.sqrt(math.log2(math.e)) / radial_width
golden_turn = math.pi * (3.0 - math.sqrt(5.0))


def direction_rows(total):
    order = np.arange(total, dtype=np.float64)
    height = 1.0 - (2.0 * order + 1.0) / total
    radius = np.sqrt(1.0 - height * height)
    turning = order * golden_turn
    table = np.zeros((-(-total // 8) * 8, 128), np.float32)
    table[:total, :3] = np.stack([radius * np.cos(turning), radius * np.sin(turning), height], axis=1)
    return table


def pitch_of(count):
    return count + 1


def store_powers(table, coords, half, tile, cosines, sines):
    base = (
        table[:, 0:1] * coords[0:1] + table[:, 1:2] * coords[1:2] + table[:, 2:3] * coords[2:3]
    ) * (0.5 / half)
    count = table.shape[0]
    pitch = pitch_of(count)
    powers = {1: (jnp.cos(base), jnp.sin(base))}
    for n in range(2, 9):
        (ca, sa), (cb, sb) = powers[n // 2], powers[n - n // 2]
        powers[n] = (ca * cb - sa * sb, sa * cb + ca * sb)
    for n in range(1, 9):
        rows = slice((n - 1) * pitch, (n - 1) * pitch + count)
        cosines[tile, rows, :] = powers[n][0]
        sines[tile, rows, :] = powers[n][1]


def rotated(features, lanes, direction, pitch, half, cosines, sines, tile):
    rows = pl.ds(direction, 8, stride=pitch)
    last = pl.ds(7 * pitch + direction, 1)
    cosine, sine = cosines[tile, rows, :], sines[tile, rows, :]
    step_c = jnp.broadcast_to(cosines[tile, last, :], cosine.shape)
    step_s = jnp.broadcast_to(sines[tile, last, :], sine.shape)
    double = 2.0 * step_c
    older = None
    turned = []
    for first in range(0, half, 8):
        if first == 8:
            older = (cosine, sine)
            cosine, sine = cosine * step_c - sine * step_s, sine * step_c + cosine * step_s
        elif first > 8:
            held = (cosine, sine)
            cosine, sine = double * cosine - older[0], double * sine - older[1]
            older = held
        turned.append((cosine, sine))
    low, high = [], []
    for first in range(0, half, 16):
        pair = turned[first // 8 : first // 8 + 2]
        cosine, sine = [
            jnp.concatenate([both[which] for both in pair], axis=0).astype(jnp.bfloat16)
            for which in range(2)
        ]
        a = features[first : first + 16, lanes]
        b = features[half + first : half + first + 16, lanes]
        low.append(a * cosine - b * sine)
        high.append(b * cosine + a * sine)
    return jnp.concatenate(low + high, axis=0)


def vmem(count):
    return [pl.BlockSpec(memory_space=pltpu.VMEM)] * count


def bits_of(count):
    return count.bit_length() - 1


def message_kernel(
    cells, dirs, slot_cap, per_owner, entries_ref, counts_ref, places_ref, gains_ref, update_ref, features_ref,
    received_ref, near, raw, scaled, face_out, face_in, parcels, local_sem, face_send, face_recv, send_sems, recv_sems,
):
    me = lax.axis_index("cell")
    turn = lax.axis_index("dir")
    capacity = features_ref.shape[0]
    block, width = features_ref.shape[1], features_ref.shape[2]
    faces = H
    before, after = lax.rem(me + cells - 1, cells), lax.rem(me + 1, cells)
    own_copy = pltpu.make_async_copy(features_ref, near.at[pl.ds(0, capacity)], local_sem)
    own_copy.start()
    barrier = pltpu.get_barrier_semaphore()

    def greet(k, carried):
        pl.semaphore_signal(
            barrier, inc=1, device_id={"cell": lax.rem(me + k, cells)}, device_id_type=pl.DeviceIdType.MESH
        )
        return carried

    lax.fori_loop(1, cells, greet, 0)
    axes = places_ref.shape[0]
    for axis in range(axes):
        lifted = places_ref[axis].astype(jnp.float32)
        raw[axis, 0:capacity, :] = lifted
        scaled[axis, 0:capacity, :] = lifted * radial_scale
        face_out[axis * faces : (axis + 1) * faces, :] = lifted[0:faces]
    pl.semaphore_wait(barrier, cells - 1)

    face_copies = []
    for side, device in ((0, after), (1, before)):
        landing = pl.ds(capacity + side * faces, faces)
        pairs = (
            (features_ref.at[pl.ds(0, faces)], near.at[landing]),
            (face_out, face_in.at[side]),
        )
        for kind, (source, target) in enumerate(pairs):
            copy = pltpu.make_async_remote_copy(
                src_ref=source, dst_ref=target, send_sem=face_send.at[side, kind],
                recv_sem=face_recv.at[side, kind], device_id={"cell": device},
                device_id_type=pl.DeviceIdType.MESH,
            )
            copy.start()
            face_copies.append(copy)

    first_live = lax.fori_loop(0, me, lambda c, total: total + counts_ref[c], jnp.int32(0))
    own_count = counts_ref[me]
    first_slot = lax.rem(turn + dirs * cells * capacity - first_live, dirs)
    period = cells * slot_cap
    own_copy.wait()
    for copy in face_copies:
        copy.wait_recv()
    for side, shift in ((0, -slab_width), (1, slab_width)):
        for axis in range(axes):
            moved = face_in[side, axis * faces : (axis + 1) * faces, :]
            if axis == 0:
                moved = moved + shift
            scaled[axis, capacity + side * faces : capacity + (side + 1) * faces, :] = moved * radial_scale

    centers = [(2.0 + 2.0 * k) * radial_scale for k in range(gains_ref.shape[0])]
    row = lax.broadcasted_iota(jnp.int32, (16, width), 0)

    def serve(step, carried):
        item = step
        destination = lax.rem(me + 1 + step // per_owner, cells)
        lane = lax.rem(step, per_owner)
        if per_owner * dirs == slot_cap:
            wanted = destination * slot_cap + lane * dirs + turn
        else:
            wanted = destination * slot_cap + lane
        offset = lax.rem(wanted + period * capacity * cells - first_live, period)
        mine = (offset < own_count) & (lax.rem(offset + dirs - first_slot, dirs) == 0)
        slot = jnp.where(mine, offset, 0)
        columns = []
        for axis in range(axes):
            line = jnp.broadcast_to(scaled[axis, pl.ds(slot, 1), :], (block, block))
            columns.append(line.T)
        features, distances = [], []
        for j in range(entries_ref.shape[0]):
            entry = entries_ref[j, slot]
            place = jnp.where(entry < faces, capacity + entry, jnp.where(entry < faces + capacity, entry - faces, entry))
            features.append(near[place])
            square = None
            for axis in range(axes):
                differ = columns[axis] - scaled[axis, pl.ds(place, 1), :]
                term = differ * differ
                square = term if square is None else square + term
            distances.append(jnp.sqrt(square))
        message = None
        stacked = jnp.concatenate(features, axis=0)
        for k, center in enumerate(centers):
            parts = []
            for distance in distances:
                away = distance - center
                parts.append(jnp.exp2(-(away * away)).astype(jnp.bfloat16))
            summed = jnp.dot(jnp.concatenate(parts, axis=1), stacked, preferred_element_type=jnp.float32)
            summed = summed * gains_ref[k : k + 1, :]
            message = summed if message is None else message + summed
        activated = (message / (1.0 + jnp.exp(-message))).astype(jnp.bfloat16)
        updated = near[slot].astype(jnp.float32) + jnp.dot(
            activated, update_ref[...], preferred_element_type=jnp.float32
        )
        parcels[item, 0:block, :] = updated.astype(jnp.bfloat16)
        held = jnp.zeros((16, width), jnp.float32)
        for axis in range(axes):
            held = jnp.where(row == axis, raw[axis, pl.ds(slot, 1), :], held)
        parcels[item, block : block + 16, :] = held.astype(jnp.bfloat16)

        @pl.when(step < (cells - 1) * per_owner)
        def _():
            pltpu.make_async_remote_copy(
                src_ref=parcels.at[item], dst_ref=received_ref.at[me * per_owner + lane],
                send_sem=send_sems.at[step], recv_sem=recv_sems.at[step],
                device_id={"cell": destination}, device_id_type=pl.DeviceIdType.MESH,
            ).start()

        return carried

    lax.fori_loop(0, cells * per_owner, serve, 0)
    for lane in range(per_owner):
        received_ref[me * per_owner + lane] = parcels[(cells - 1) * per_owner + lane]
    for copy in face_copies:
        copy.wait_send()

    def settle(step, carried):
        lane = lax.rem(step, per_owner)
        source = lax.rem(me + cells - 1 - step // per_owner, cells)
        copy = pltpu.make_async_remote_copy(
            src_ref=parcels.at[step], dst_ref=received_ref.at[source * per_owner + lane],
            send_sem=send_sems.at[step], recv_sem=recv_sems.at[step],
            device_id={"cell": lax.rem(me + 1 + step // per_owner, cells)},
            device_id_type=pl.DeviceIdType.MESH,
        )
        copy.wait_recv()
        copy.wait_send()
        return carried

    lax.fori_loop(0, (cells - 1) * per_owner, settle, 0)


def deal_updates(entries, counts, places, gains, w_update, features, cells, dirs, slot_cap, per_owner):
    capacity, block, width = features.shape
    axes = places.shape[0]
    total = capacity + 2 * H
    items = cells * per_owner
    return pl.pallas_call(
        functools.partial(message_kernel, cells, dirs, slot_cap, per_owner),
        out_shape=jax.ShapeDtypeStruct((items, block + 16, width), jnp.bfloat16),
        in_specs=[pl.BlockSpec(memory_space=pltpu.SMEM)] * 2 + vmem(3) + [pl.BlockSpec(memory_space=pl.ANY)],
        out_specs=pl.BlockSpec(memory_space=pltpu.VMEM),
        scratch_shapes=[
            pltpu.VMEM((total, block, width), jnp.bfloat16),
            pltpu.VMEM((axes, capacity, width), jnp.float32),
            pltpu.VMEM((axes, total, width), jnp.float32),
            pltpu.VMEM((axes * H, width), jnp.float32),
            pltpu.VMEM((2, axes * H, width), jnp.float32),
            pltpu.VMEM((items, block + 16, width), jnp.bfloat16),
            pltpu.SemaphoreType.DMA,
            pltpu.SemaphoreType.DMA((2, 2)),
            pltpu.SemaphoreType.DMA((2, 2)),
            pltpu.SemaphoreType.DMA((items,)),
            pltpu.SemaphoreType.DMA((items,)),
        ],
        compiler_params=pltpu.CompilerParams(collective_id=1, has_side_effects=True),
        cost_estimate=pl.CostEstimate(flops=20_000_000_000, bytes_accessed=4_000_000, transcendentals=0),
        name="deal_updates",
    )(entries, counts, places, gains, w_update, features)


def reduce_stages(bits):
    stages = [["dir", 0]]
    rest = list(range(1, bits))
    while rest:
        stages.append(rest[:3])
        rest = rest[3:]
    return stages


def direction_groups(total, width, devices, wanted=12):
    unit = 16 * devices
    least = max(1, unit // width)
    size = max(least, wanted // least * least)
    groups, row = [], 0
    for first in range(0, total, size):
        count = min(size, total - first)
        rows = -(-count * width // unit) * unit
        groups.append((row, rows, first, count))
        row += rows
    return groups, row


def attend_kernel(
    cells, dirs, slot_cap, per_owner, dealt, groups, scale, counts_ref, table_ref, received_ref, projections_ref, output_ref, out_ref,
    kept, places, came, came_places, keys, values, queries, cosines, sines, total, sent, landed, states, turned_queries, mixed,
    swap_send, swap_recv, reduce_send, reduce_recv, gather_send, gather_recv,
):
    me, turn = lax.axis_index("cell"), lax.axis_index("dir")
    bits = bits_of(cells)
    blocks, block, width = kept.shape
    half = width // 2
    count = table_ref.shape[0]
    pitch = pitch_of(count)
    axes = 3
    stages = reduce_stages(bits)

    def bit_of(name):
        return turn if name == "dir" else lax.rem(me // (1 << name), 2)

    def device_of(flips):
        cell, side = me, turn
        for name in flips:
            if name == "dir":
                side = 1 - turn
            else:
                cell = cell + (1 - 2 * bit_of(name)) * (1 << name)
        return {"cell": cell, "dir": side}

    def pattern(stage, flips):
        value = 0
        for at, name in enumerate(stage):
            bit = bit_of(name)
            value = value + ((1 - bit) if name in flips else bit) * (1 << at)
        return value

    def peers(stage):
        return [
            [name for at, name in enumerate(stage) if (mask >> at) % 2] for mask in range(1, 1 << len(stage))
        ]

    def copy_to(flips, source, target, send_sem, recv_sem):
        copy = pltpu.make_async_remote_copy(
            src_ref=source, dst_ref=target, send_sem=send_sem, recv_sem=recv_sem,
            device_id=device_of(flips), device_id_type=pl.DeviceIdType.MESH,
        )
        copy.start()
        return copy

    barrier = pltpu.get_barrier_semaphore()
    greeted = 0
    for stage in stages:
        for flips in peers(stage):
            pl.semaphore_signal(
                barrier, inc=1, device_id=device_of(flips), device_id_type=pl.DeviceIdType.MESH
            )
            greeted += 1

    for m in range(blocks):
        target = m * dirs + turn if dealt else turn * blocks + m
        live = (target // slot_cap * cells + me) * slot_cap + lax.rem(target, slot_cap)

        def tally(c, carried):
            end, source = carried
            end = end + counts_ref[c]
            return end, source + (end <= live).astype(jnp.int32)

        _, source = lax.fori_loop(0, cells, tally, (jnp.int32(0), jnp.int32(0)))
        source = jnp.minimum(source, cells - 1)
        at = source * per_owner + lax.rem(target, slot_cap) // dirs if dealt else m
        kept[m] = received_ref[at, 0:block, :]
        lifted = received_ref[at, block : block + 16, :].astype(jnp.float32)
        row = lax.broadcasted_iota(jnp.int32, lifted.shape, 0)
        lifted = lifted + jnp.where(row == 0, slab_width * source.astype(jnp.float32), 0.0)
        places[m] = lifted[0:8]
    running = []
    pl.semaphore_wait(barrier, greeted)
    shared = blocks // dirs
    if dealt:
        away = pl.ds((1 - turn) * shared, shared)
        running.append(copy_to(["dir"], kept.at[away], came, swap_send.at[0], swap_recv.at[0]))
        running.append(copy_to(["dir"], places.at[away], came_places, swap_send.at[1], swap_recv.at[1]))
    swapped = list(running)

    rows = kept[...].reshape(blocks * block, width)
    keys[...] = lax.dot_general(
        projections_ref[:, width : 2 * width].T, rows, (((1,), (1,)), ((), ())), preferred_element_type=jnp.float32
    ).astype(jnp.bfloat16)
    values[...] = jnp.dot(rows, projections_ref[:, 2 * width :], preferred_element_type=jnp.float32).astype(jnp.bfloat16)

    def powers_of(tile, carried):
        store_powers(table_ref[...], places[tile], half, tile, cosines, sines)
        return carried

    lax.fori_loop(0, blocks, powers_of, 0)

    def lanes_of(tile):
        return slice(tile * block, (tile + 1) * block)

    def key_states(group):
        row, rows, first, number = group

        def advance(turn_index, carried):
            direction = first + 2 * turn_index
            parts = []
            for j in range(2):
                parts.append(jnp.concatenate(
                    [
                        rotated(keys, lanes_of(tile), direction + j, pitch, half, cosines, sines, tile)
                        for tile in range(blocks)
                    ], axis=1,
                ))
            at = pl.ds(pl.multiple_of(row + turn_index * 2 * width, 2 * width), 2 * width)
            state = jnp.dot(jnp.concatenate(parts, axis=0), values[...], preferred_element_type=jnp.float32)
            total[at, :] = state
            sent[0][at, :] = state.astype(jnp.bfloat16)
            return carried

        lax.fori_loop(0, number // 2, advance, 0)
        if number * width < rows:
            rest = slice(row + number * width, row + rows)
            total[rest, :] = jnp.zeros((rows - number * width, width), jnp.float32)
            sent[0][rest, :] = jnp.zeros((rows - number * width, width), jnp.bfloat16)

    spans = {}
    flying = {}
    shares = [1]
    for stage in stages:
        shares.append(shares[-1] * (1 << len(stage)))

    def issue(g, step):
        row, rows = groups[g][:2]
        if step < len(stages):
            stage = stages[step]
            if step == 0:
                spans[g] = (row, rows)
            begin, length = spans[g]
            piece = length // (1 << len(stage))
            base = row // shares[step]
            copies = []
            for k, flips in enumerate(peers(stage)):
                source = pl.multiple_of(base + pattern(stage, flips) * piece, 16)
                copies.append(copy_to(
                    flips, sent[step].at[pl.ds(source, piece), :],
                    landed[step].at[k, pl.ds(row // shares[step + 1], piece), :],
                    reduce_send[step].at[g, k], reduce_recv[step].at[g, k],
                ))
        else:
            step_at = 2 * len(stages) - 1 - step
            stage = stages[step_at]
            begin, length = spans[g]
            at = pl.ds(pl.multiple_of(begin, 16), length)
            copies = [
                copy_to(
                    flips, states.at[at, :], states.at[at, :],
                    gather_send[step_at].at[g, k], gather_recv[step_at].at[g, k],
                )
                for k, flips in enumerate(peers(stage))
            ]
        flying[g, step] = copies
        running.extend(copies)

    def finish(g, step):
        for copy in flying[g, step]:
            copy.wait_recv()
        row, rows = groups[g][:2]
        begin, length = spans[g]
        if step < len(stages):
            stage = stages[step]
            piece = length // (1 << len(stage))
            begin = pl.multiple_of(begin + pattern(stage, []) * piece, 16)
            summed = total[pl.ds(begin, piece), :]
            for k in range(len(peers(stage))):
                summed = summed + landed[step][k, row // shares[step + 1] : row // shares[step + 1] + piece, :].astype(jnp.float32)
            if step + 1 < len(stages):
                total[pl.ds(begin, piece), :] = summed
                sent[step + 1][row // shares[step + 1] : row // shares[step + 1] + piece, :] = summed.astype(jnp.bfloat16)
            else:
                states[pl.ds(begin, piece), :] = summed.astype(jnp.bfloat16)
            spans[g] = (begin, piece)
        else:
            stage = stages[2 * len(stages) - 1 - step]
            spans[g] = (begin - pattern(stage, []) * length, length * (1 << len(stage)))

    def query_tile(tile):
        def advance(direction, carried):
            at = pl.ds(pl.multiple_of(direction * width, width), width)
            turned_queries[at, lanes_of(tile)] = rotated(
                queries, lanes_of(tile), direction, pitch, half, cosines, sines, tile
            )
            return carried

        lax.fori_loop(0, DIRS, advance, 0)

    def prepare_queries():
        for copy in swapped:
            copy.wait_recv()
        if dealt:
            held = pl.ds(turn * shared, shared)
            rows = jnp.concatenate(
                [kept[held].reshape(shared * block, width), came[...].reshape(shared * block, width)], axis=0
            )
        else:
            rows = kept[...].reshape(blocks * block, width)
        queries[...] = lax.dot_general(
            projections_ref[:, :width].T, rows, (((1,), (1,)), ((), ())), preferred_element_type=jnp.float32
        ).astype(jnp.bfloat16)
        if dealt:
            def again(tile, carried):
                store_powers(table_ref[...], places[turn * shared + tile], half, tile, cosines, sines)
                store_powers(table_ref[...], came_places[tile], half, shared + tile, cosines, sines)
                return carried

            lax.fori_loop(0, shared, again, 0)

    steps = 2 * len(stages)
    done = {g: -1 for g in range(len(groups))}

    def progress(g):
        if done[g] >= 0:
            finish(g, done[g])
        done[g] += 1
        if done[g] < steps:
            issue(g, done[g])

    slots = [functools.partial(key_states, group) for group in groups]
    slots.append(prepare_queries)
    slots += [functools.partial(query_tile, tile) for tile in range(blocks)]
    lags = [0] + [2, 3] * len(stages)
    due = {}
    for g in range(len(groups)):
        at = g
        for step in range(steps + 1):
            lag = 0 if step == 0 else (2 if step in (1, steps) else 3)
            at += lag
            due.setdefault(min(at, len(slots) + steps), []).append(g)
    for at, slot in enumerate(slots):
        slot()
        for g in due.get(at, []):
            progress(g)
    started = False
    for step in range(steps + 1):
        for g in range(len(groups)):
            if done[g] < step:
                progress(g)
    for g, (row, rows, first, number) in enumerate(groups):
        flipped = jnp.concatenate(
            [states[row + d * width : row + (d + 1) * width, :].T for d in range(number)], axis=1
        )
        term = jnp.dot(
            flipped, turned_queries[first * width : (first + number) * width, :],
            preferred_element_type=jnp.float32,
        )
        mixed[...] = term if g == 0 else mixed[...] + term
    for tile in range(blocks):
        if dealt:
            place = 2 * tile + turn if tile < shared else 2 * (tile - shared) + 1 - turn
        else:
            place = tile
        part = (mixed[:, lanes_of(tile)] * scale).T.astype(jnp.bfloat16)
        out_ref[place] = jnp.dot(part, output_ref[...], preferred_element_type=jnp.float32).astype(jnp.bfloat16)
    for copy in running:
        copy.wait_send()


def attend(counts, received, projections, w_output, cells, dirs, slot_cap, per_owner, dealt, blocks, block, scale):
    width = w_output.shape[0]
    stages = reduce_stages(bits_of(cells))
    groups, padded = direction_groups(DIRS, width, cells * dirs)
    table = jnp.asarray(direction_rows(DIRS))
    count = table.shape[0]
    pitch = pitch_of(count)
    shares = [1]
    for stage in stages:
        shares.append(shares[-1] * (1 << len(stage)))
    sizes = [(1 << len(stage)) - 1 for stage in stages]
    power_rows = -(-(7 * pitch + count) // 8) * 8

    def sems():
        return [pltpu.SemaphoreType.DMA((len(groups), size)) for size in sizes]

    return pl.pallas_call(
        functools.partial(attend_kernel, cells, dirs, slot_cap, per_owner, dealt, groups, scale),
        out_shape=jax.ShapeDtypeStruct((blocks, block, width), jnp.bfloat16),
        in_specs=[pl.BlockSpec(memory_space=pltpu.SMEM)] + vmem(4),
        out_specs=pl.BlockSpec(memory_space=pltpu.VMEM),
        scratch_shapes=[
            pltpu.VMEM((blocks, block, width), jnp.bfloat16),
            pltpu.VMEM((blocks, 8, width), jnp.float32),
            pltpu.VMEM((blocks // dirs, block, width), jnp.bfloat16),
            pltpu.VMEM((blocks // dirs, 8, width), jnp.float32),
            pltpu.VMEM((width, blocks * block), jnp.bfloat16),
            pltpu.VMEM((blocks * block, width), jnp.bfloat16),
            pltpu.VMEM((width, blocks * block), jnp.bfloat16),
            pltpu.VMEM((blocks, power_rows, width), jnp.float32),
            pltpu.VMEM((blocks, power_rows, width), jnp.float32),
            pltpu.VMEM((padded, width), jnp.float32),
            [pltpu.VMEM((padded // share, width), jnp.bfloat16) for share in shares[:-1]],
            [pltpu.VMEM((size, padded // share, width), jnp.bfloat16) for size, share in zip(sizes, shares[1:])],
            pltpu.VMEM((padded, width), jnp.bfloat16),
            pltpu.VMEM((DIRS * width, blocks * block), jnp.bfloat16),
            pltpu.VMEM((width, blocks * block), jnp.float32),
            pltpu.SemaphoreType.DMA((2,)),
            pltpu.SemaphoreType.DMA((2,)),
            sems(), sems(), sems(), sems(),
        ],
        compiler_params=pltpu.CompilerParams(collective_id=0, has_side_effects=True),
        cost_estimate=pl.CostEstimate(flops=40_000_000_000, bytes_accessed=4_000_000, transcendentals=0),
        name="attend",
    )(counts, table, received, projections, w_output)


def per_device(
    atom_features, positions, neighbours, counts, filter_gains, w_update, projections, w_output
):
    cells = lax.axis_size("cell")
    cell_index = lax.axis_index("cell")
    dirs_count = lax.axis_size("dir")
    dir_index = lax.axis_index("dir")
    capacity, block_atoms, width = atom_features.shape
    balanced_blocks = capacity // 2
    share_blocks = balanced_blocks // dirs_count
    slot_cap = max(1, 2 * balanced_blocks // cells)
    whole_rounds = slot_cap % dirs_count == 0
    per_owner = slot_cap // dirs_count if whole_rounds else slot_cap
    received = deal_updates(
        neighbours.T, counts, jnp.transpose(positions, (1, 0, 2)), filter_gains, w_update, atom_features,
        cells, dirs_count, slot_cap, per_owner,
    )
    if not whole_rounds:
        count_ends = jnp.cumsum(counts)
        target = jnp.arange(balanced_blocks, dtype=jnp.int32)
        global_index = (target // slot_cap * cells + cell_index) * slot_cap + target % slot_cap
        source = jnp.sum((count_ends[None, :] <= global_index[:, None]).astype(jnp.int32), axis=1)
        rows = received[source * per_owner + target % slot_cap]
        balanced = rows
        for hop in range(1, dirs_count):
            other = lax.ppermute(rows, "dir", [(i, (i + hop) % dirs_count) for i in range(dirs_count)])
            held = global_index % dirs_count == (dir_index - hop) % dirs_count
            balanced = jnp.where(held[:, None, None], other, balanced)
        received = lax.dynamic_slice_in_dim(balanced, dir_index * share_blocks, share_blocks, 0)
    mix_scale = 1.0 / math.sqrt(DIRS * cells * balanced_blocks * block_atoms * width)
    return attend(
        counts, received, projections, w_output, cells, dirs_count, slot_cap, per_owner, whole_rounds,
        share_blocks, block_atoms, mix_scale,
    )


def solution(mesh):
    placed = (
        P("cell", None, None),
        P("cell", None, None),
        P("cell", None),
        P(),
        P(),
        P(),
        P(),
        P(),
    )
    return jax.shard_map(
        per_device,
        mesh=mesh,
        in_specs=placed,
        out_specs=P(("cell", "dir"), None, None),
        check_vma=False,
    )
```

time: 109 us -> 88.7 us (0.81)
  Pallas kernels: 94.1 us -> 86.8 us
  local copies, waits for them, and re-layouts: 6.77 us -> 1.67 us
  starting transfers between devices: 3.23 us -> 0 us
  other arithmetic: 2.79 us -> 0 us
  matrix products: 1.96 us -> 0 us
    pallas_call x5 -> x1, Pallas kernels: 66.2 us -> 58.9 us  [attend(): pl.pallas_call(functools.partial(attend_kernel, cells, dirs, slot_cap, pe...]
    ppermute x2 -> x0, starting transfers between devices: 3.23 us -> none  [the longest x1 1.68 us: per_device(): lax.ppermute(away, 'dir', [(i, (i + hop) % dirs_count) for i in range(dir...]
    gather x3 -> x0, local copies, waits for them, and re-layouts: 2.37 us -> none  [the longest x1 1.67 us: per_device(): rows = received[dealt_to(source, dir_index) * per_owner + within]]
    dot_general x1 -> x0, matrix products: 1.96 us -> none  [per_device(): jnp.dot(mixed, w_output, preferred_element_type=jnp.float32)]
  transfers between devices with their start and end apart: 2 -> 0, of which waited for: 0 -> 0; matrix products, arithmetic and copies ran while one was open for 3% -> 0% of each run, Pallas kernels for 54% -> 0%
where the time goes in v2:
time: 88.7 us; the launch traced here: 88.5 us
  Pallas kernels  86.8 us (98%)
  local copies, waits for them, and re-layouts  1.67 us (2%)
    pallas_call x1, Pallas kernels, attend(): pl.pallas_call(functools.partial(attend_kernel, cells, dirs, slot_cap, pe...  58.9 us
    pallas_call x1, Pallas kernels, deal_updates(): pl.pallas_call(functools.partial(message_kernel, cells, dirs, slot_cap, p...  27.9 us

profile of v2, /device:TPU:0, one launch (start us, length us, event | category | flops | bytes accessed | tf_op | source)
XLA Modules:
  0.0 88.5 jit_solution(12992049836051281537)
XLA Ops:
  0.0 27.9 %deal_updates.1.received_ref = bf16[16,144,128]{2,1,0:T(8,128)(2,1)} custom-call(s32[4,32]{1,0:T(4,128)} %bitcast.3, s32[16]{0:T(128)} %counts_ref.3, bf16[3,32,128]{2,1,0:T(8,128)(2,1)} %bitcast.2, f32[8,128]{1,0:T(8,128)} %gains_ref.1, bf16[128,128]{1,0:T(8,128)(2,1)} %update_ref.1, bf16[32,128,128]{2,1,0:T(8,128)(2,1)} %features_ref.1), custom_call_target="tpu_custom_call" | custom-call | flops 20000000000 | bytes 4000000 | tf_op jit(solution)/shard_map/deal_updates/pallas_call | solution.py:237
  27.9 58.9 %attend.1 = bf16[8,128,128]{2,1,0:T(8,128)(2,1)} custom-call(s32[16]{0:T(128)} %counts_ref.3, f32[56,128]{1,0:T(8,128)} %constant.2.clone.table_ref, bf16[16,144,128]{2,1,0:T(8,128)(2,1)} %deal_updates.1.received_ref, bf16[128,384]{1,0:T(8,128)(2,1)} %projections_ref.1, bf16[128,128]{1,0:T(8,128)(2,1)} %output_ref.1), custom_call_target="tpu_custom_call" | custom-call | flops 40000000000 | bytes 4000000 | tf_op jit(solution)/shard_map/attend/pallas_call | solution.py:561
  86.8 1.7 %copy.11 = bf16[8,128,128]{2,1,0:T(8,128)(2,1)} copy(bf16[8,128,128]{2,1,0:T(8,128)(2,1)} %attend.1) | data formatting | bytes 524288

commit v3 on v2

--- a/solution.py
+++ b/solution.py
@@ -49,12 +49,15 @@
         sines[tile, rows, :] = powers[n][1]
 
 
-def rotated(features, lanes, direction, pitch, half, cosines, sines, tile):
+def rotated(features, lanes, direction, pitch, half, cosines, sines, tiles):
+    def across(held, rows):
+        return jnp.concatenate([held[tile, rows, :] for tile in tiles], axis=1)
+
     rows = pl.ds(direction, 8, stride=pitch)
     last = pl.ds(7 * pitch + direction, 1)
-    cosine, sine = cosines[tile, rows, :], sines[tile, rows, :]
-    step_c = jnp.broadcast_to(cosines[tile, last, :], cosine.shape)
-    step_s = jnp.broadcast_to(sines[tile, last, :], sine.shape)
+    cosine, sine = across(cosines, rows), across(sines, rows)
+    step_c = jnp.broadcast_to(across(cosines, last), cosine.shape)
+    step_s = jnp.broadcast_to(across(sines, last), sine.shape)
     double = 2.0 * step_c
     older = None
     turned = []
@@ -176,14 +179,14 @@
                 differ = columns[axis] - scaled[axis, pl.ds(place, 1), :]
                 term = differ * differ
                 square = term if square is None else square + term
-            distances.append(jnp.sqrt(square))
+            distances.append(square * lax.rsqrt(jnp.maximum(square, 1e-30)))
         message = None
         stacked = jnp.concatenate(features, axis=0)
         for k, center in enumerate(centers):
             parts = []
             for distance in distances:
-                away = distance - center
-                parts.append(jnp.exp2(-(away * away)).astype(jnp.bfloat16))
+                away = (distance - center).astype(jnp.bfloat16)
+                parts.append(jnp.exp2(-(away * away)))
             summed = jnp.dot(jnp.concatenate(parts, axis=1), stacked, preferred_element_type=jnp.float32)
             summed = summed * gains_ref[k : k + 1, :]
             message = summed if message is None else message + summed
@@ -259,15 +262,15 @@
 
 
 def reduce_stages(bits):
-    stages = [["dir", 0]]
-    rest = list(range(1, bits))
+    stages = [[0], ["dir", 1]]
+    rest = list(range(2, bits))
     while rest:
-        stages.append(rest[:3])
-        rest = rest[3:]
+        stages.append(rest[:2])
+        rest = rest[2:]
     return stages
 
 
-def direction_groups(total, width, devices, wanted=12):
+def direction_groups(total, width, devices, wanted=8):
     unit = 16 * devices
     least = max(1, unit // width)
     size = max(least, wanted // least * least)
@@ -376,19 +379,23 @@
     def lanes_of(tile):
         return slice(tile * block, (tile + 1) * block)
 
+    def turned_by(features, direction):
+        return jnp.concatenate(
+            [
+                rotated(
+                    features, slice(tile * block, (tile + 2) * block), direction, pitch, half, cosines, sines,
+                    (tile, tile + 1),
+                )
+                for tile in range(0, blocks, 2)
+            ], axis=1,
+        )
+
     def key_states(group):
         row, rows, first, number = group
 
         def advance(turn_index, carried):
             direction = first + 2 * turn_index
-            parts = []
-            for j in range(2):
-                parts.append(jnp.concatenate(
-                    [
-                        rotated(keys, lanes_of(tile), direction + j, pitch, half, cosines, sines, tile)
-                        for tile in range(blocks)
-                    ], axis=1,
-                ))
+            parts = [turned_by(keys, direction + j) for j in range(2)]
             at = pl.ds(pl.multiple_of(row + turn_index * 2 * width, 2 * width), 2 * width)
             state = jnp.dot(jnp.concatenate(parts, axis=0), values[...], preferred_element_type=jnp.float32)
             total[at, :] = state
@@ -461,15 +468,29 @@
             stage = stages[2 * len(stages) - 1 - step]
             spans[g] = (begin - pattern(stage, []) * length, length * (1 << len(stage)))
 
-    def query_tile(tile):
+    def turn_queries(group):
+        first, number = group[2:]
+
         def advance(direction, carried):
             at = pl.ds(pl.multiple_of(direction * width, width), width)
-            turned_queries[at, lanes_of(tile)] = rotated(
-                queries, lanes_of(tile), direction, pitch, half, cosines, sines, tile
-            )
+            turned_queries[at, :] = turned_by(queries, direction)
             return carried
 
-        lax.fori_loop(0, DIRS, advance, 0)
+        lax.fori_loop(first, first + number, advance, 0)
+
+    def mix(g):
+        row, rows, first, number = groups[g]
+        flipped = jnp.concatenate(
+            [states[row + d * width : row + (d + 1) * width, :].T for d in range(number)], axis=1
+        )
+        term = jnp.dot(
+            flipped, turned_queries[first * width : (first + number) * width, :],
+            preferred_element_type=jnp.float32,
+        )
+        mixed[...] = mixed[...] + term if mixed_groups else term
+        mixed_groups.append(g)
+
+    mixed_groups = []
 
     def prepare_queries():
         for copy in swapped:
@@ -504,33 +525,28 @@
 
     slots = [functools.partial(key_states, group) for group in groups]
     slots.append(prepare_queries)
-    slots += [functools.partial(query_tile, tile) for tile in range(blocks)]
+    slots += [functools.partial(turn_queries, group) for group in groups]
     lags = [0] + [2, 3] * len(stages)
     due = {}
     for g in range(len(groups)):
         at = g
         for step in range(steps + 1):
-            lag = 0 if step == 0 else (2 if step in (1, steps) else 3)
+            lag = 0 if step == 0 else (1 if step in (1, steps) else 3)
             at += lag
             due.setdefault(min(at, len(slots) + steps), []).append(g)
     for at, slot in enumerate(slots):
         slot()
         for g in due.get(at, []):
             progress(g)
-    started = False
+    for g in range(len(groups)):
+        if done[g] == steps:
+            mix(g)
     for step in range(steps + 1):
         for g in range(len(groups)):
             if done[g] < step:
                 progress(g)
-    for g, (row, rows, first, number) in enumerate(groups):
-        flipped = jnp.concatenate(
-            [states[row + d * width : row + (d + 1) * width, :].T for d in range(number)], axis=1
-        )
-        term = jnp.dot(
-            flipped, turned_queries[first * width : (first + number) * width, :],
-            preferred_element_type=jnp.float32,
-        )
-        mixed[...] = term if g == 0 else mixed[...] + term
+                if done[g] == steps:
+                    mix(g)
     for tile in range(blocks):
         if dealt:
             place = 2 * tile + turn if tile < shared else 2 * (tile - shared) + 1 - turn

time: 88.7 us -> 69.2 us (0.78)
  Pallas kernels: 86.8 us -> 67.2 us
    pallas_call x1, Pallas kernels: 58.9 us -> 40.1 us  [attend(): pl.pallas_call(functools.partial(attend_kernel, cells, dirs, slot_cap, pe...]
where the time goes in v3:
time: 69.2 us; the launch traced here: 68.9 us
  Pallas kernels  67.2 us (97%)
  local copies, waits for them, and re-layouts  1.67 us (2%)
    pallas_call x1, Pallas kernels, attend(): pl.pallas_call(functools.partial(attend_kernel, cells, dirs, slot_cap, pe...  40.1 us
    pallas_call x1, Pallas kernels, deal_updates(): pl.pallas_call(functools.partial(message_kernel, cells, dirs, slot_cap, p...  27.2 us
    unnamed x1, local copies, waits for them, and re-layouts  1.67 us

profile of v3, /device:TPU:0, one launch (start us, length us, event | category | flops | bytes accessed | tf_op | source)
XLA Modules:
  0.0 68.9 jit_solution(14168883837306143040)
XLA Ops:
  0.0 27.2 %deal_updates.1.received_ref = bf16[16,144,128]{2,1,0:T(8,128)(2,1)} custom-call(s32[4,32]{1,0:T(4,128)} %bitcast.3, s32[16]{0:T(128)} %counts_ref.3, bf16[3,32,128]{2,1,0:T(8,128)(2,1)} %bitcast.2, f32[8,128]{1,0:T(8,128)} %gains_ref.1, bf16[128,128]{1,0:T(8,128)(2,1)} %update_ref.1, bf16[32,128,128]{2,1,0:T(8,128)(2,1)} %features_ref.1), custom_call_target="tpu_custom_call" | custom-call | flops 20000000000 | bytes 4000000 | tf_op jit(solution)/shard_map/deal_updates/pallas_call | solution.py:240
  27.2 40.1 %attend.1 = bf16[8,128,128]{2,1,0:T(8,128)(2,1)} custom-call(s32[16]{0:T(128)} %counts_ref.3, f32[56,128]{1,0:T(8,128)} %constant.2.clone.table_ref, bf16[16,144,128]{2,1,0:T(8,128)(2,1)} %deal_updates.1.received_ref, bf16[128,384]{1,0:T(8,128)(2,1)} %projections_ref.1, bf16[128,128]{1,0:T(8,128)(2,1)} %output_ref.1), custom_call_target="tpu_custom_call" | custom-call | flops 40000000000 | bytes 4000000 | tf_op jit(solution)/shard_map/attend/pallas_call | solution.py:577
  67.3 1.7 %copy.11 = bf16[8,128,128]{2,1,0:T(8,128)(2,1)} copy(bf16[8,128,128]{2,1,0:T(8,128)(2,1)} %attend.1) | data formatting | bytes 524288

commit v4 on v3

--- a/solution.py
+++ b/solution.py
@@ -154,9 +154,13 @@
     centers = [(2.0 + 2.0 * k) * radial_scale for k in range(gains_ref.shape[0])]
     row = lax.broadcasted_iota(jnp.int32, (16, width), 0)
 
+    def hop_of(step):
+        turn_at = step // per_owner
+        return cells // 2 + (2 * lax.rem(turn_at, 2) - 1) * ((turn_at + 1) // 2)
+
     def serve(step, carried):
         item = step
-        destination = lax.rem(me + 1 + step // per_owner, cells)
+        destination = lax.rem(me + hop_of(step), cells)
         lane = lax.rem(step, per_owner)
         if per_owner * dirs == slot_cap:
             wanted = destination * slot_cap + lane * dirs + turn
@@ -218,11 +222,11 @@
 
     def settle(step, carried):
         lane = lax.rem(step, per_owner)
-        source = lax.rem(me + cells - 1 - step // per_owner, cells)
+        source = lax.rem(me + cells - hop_of(step), cells)
         copy = pltpu.make_async_remote_copy(
             src_ref=parcels.at[step], dst_ref=received_ref.at[source * per_owner + lane],
             send_sem=send_sems.at[step], recv_sem=recv_sems.at[step],
-            device_id={"cell": lax.rem(me + 1 + step // per_owner, cells)},
+            device_id={"cell": lax.rem(me + hop_of(step), cells)},
             device_id_type=pl.DeviceIdType.MESH,
         )
         copy.wait_recv()
@@ -355,6 +359,17 @@
         row = lax.broadcasted_iota(jnp.int32, lifted.shape, 0)
         lifted = lifted + jnp.where(row == 0, slab_width * source.astype(jnp.float32), 0.0)
         places[m] = lifted[0:8]
+    rows = kept[...].reshape(blocks * block, width)
+    keys[...] = lax.dot_general(
+        projections_ref[:, width : 2 * width].T, rows, (((1,), (1,)), ((), ())), preferred_element_type=jnp.float32
+    ).astype(jnp.bfloat16)
+    values[...] = jnp.dot(rows, projections_ref[:, 2 * width :], preferred_element_type=jnp.float32).astype(jnp.bfloat16)
+
+    def powers_of(tile, carried):
+        store_powers(table_ref[...], places[tile], half, tile, cosines, sines)
+        return carried
+
+    lax.fori_loop(0, blocks, powers_of, 0)
     running = []
     pl.semaphore_wait(barrier, greeted)
     shared = blocks // dirs
@@ -363,18 +378,7 @@
         running.append(copy_to(["dir"], kept.at[away], came, swap_send.at[0], swap_recv.at[0]))
         running.append(copy_to(["dir"], places.at[away], came_places, swap_send.at[1], swap_recv.at[1]))
     swapped = list(running)
-
-    rows = kept[...].reshape(blocks * block, width)
-    keys[...] = lax.dot_general(
-        projections_ref[:, width : 2 * width].T, rows, (((1,), (1,)), ((), ())), preferred_element_type=jnp.float32
-    ).astype(jnp.bfloat16)
-    values[...] = jnp.dot(rows, projections_ref[:, 2 * width :], preferred_element_type=jnp.float32).astype(jnp.bfloat16)
-
-    def powers_of(tile, carried):
-        store_powers(table_ref[...], places[tile], half, tile, cosines, sines)
-        return carried
-
-    lax.fori_loop(0, blocks, powers_of, 0)
+    running.clear()
 
     def lanes_of(tile):
         return slice(tile * block, (tile + 1) * block)
@@ -495,21 +499,18 @@
     def prepare_queries():
         for copy in swapped:
             copy.wait_recv()
+        for copy in swapped:
+            copy.wait_send()
         if dealt:
-            held = pl.ds(turn * shared, shared)
-            rows = jnp.concatenate(
-                [kept[held].reshape(shared * block, width), came[...].reshape(shared * block, width)], axis=0
-            )
-        else:
-            rows = kept[...].reshape(blocks * block, width)
+            kept[away] = came[...]
+            places[away] = came_places[...]
         queries[...] = lax.dot_general(
-            projections_ref[:, :width].T, rows, (((1,), (1,)), ((), ())), preferred_element_type=jnp.float32
+            projections_ref[:, :width].T, kept[...].reshape(blocks * block, width), (((1,), (1,)), ((), ())),
+            preferred_element_type=jnp.float32,
         ).astype(jnp.bfloat16)
         if dealt:
             def again(tile, carried):
-                store_powers(table_ref[...], places[turn * shared + tile], half, tile, cosines, sines)
-                store_powers(table_ref[...], came_places[tile], half, shared + tile, cosines, sines)
-                return carried
+                return powers_of((1 - turn) * shared + tile, carried)
 
             lax.fori_loop(0, shared, again, 0)
 
@@ -549,7 +550,7 @@
                     mix(g)
     for tile in range(blocks):
         if dealt:
-            place = 2 * tile + turn if tile < shared else 2 * (tile - shared) + 1 - turn
+            place = dirs * (tile % shared) + tile // shared
         else:
             place = tile
         part = (mixed[:, lanes_of(tile)] * scale).T.astype(jnp.bfloat16)

time: 69.2 us -> 66.1 us (0.955)
  Pallas kernels: 67.2 us -> 64.2 us
    pallas_call x1, Pallas kernels: 40.1 us -> 35.9 us  [attend(): pl.pallas_call(functools.partial(attend_kernel, cells, dirs, slot_cap, pe...]
    pallas_call x1, Pallas kernels: 27.2 us -> 28.3 us  [deal_updates(): pl.pallas_call(functools.partial(message_kernel, cells, dirs, slot_cap, p...]
where the time goes in v4:
time: 66.1 us; the launch traced here: 65.9 us
  Pallas kernels  64.2 us (97%)
  local copies, waits for them, and re-layouts  1.67 us (3%)
    pallas_call x1, Pallas kernels, attend(): pl.pallas_call(functools.partial(attend_kernel, cells, dirs, slot_cap, pe...  35.9 us
    pallas_call x1, Pallas kernels, deal_updates(): pl.pallas_call(functools.partial(message_kernel, cells, dirs, slot_cap, p...  28.3 us
    unnamed x1, local copies, waits for them, and re-layouts  1.67 us

profile of v4, /device:TPU:0, one launch (start us, length us, event | category | flops | bytes accessed | tf_op | source)
XLA Modules:
  0.0 65.9 jit_solution(6667593033016255929)
XLA Ops:
  0.0 28.3 %deal_updates.1.received_ref = bf16[16,144,128]{2,1,0:T(8,128)(2,1)} custom-call(s32[4,32]{1,0:T(4,128)} %bitcast.3, s32[16]{0:T(128)} %counts_ref.3, bf16[3,32,128]{2,1,0:T(8,128)(2,1)} %bitcast.2, f32[8,128]{1,0:T(8,128)} %gains_ref.1, bf16[128,128]{1,0:T(8,128)(2,1)} %update_ref.1, bf16[32,128,128]{2,1,0:T(8,128)(2,1)} %features_ref.1), custom_call_target="tpu_custom_call" | custom-call | flops 20000000000 | bytes 4000000 | tf_op jit(solution)/shard_map/deal_updates/pallas_call | solution.py:244
  28.3 35.9 %attend.1 = bf16[8,128,128]{2,1,0:T(8,128)(2,1)} custom-call(s32[16]{0:T(128)} %counts_ref.3, f32[56,128]{1,0:T(8,128)} %constant.2.clone.table_ref, bf16[16,144,128]{2,1,0:T(8,128)(2,1)} %deal_updates.1.received_ref, bf16[128,384]{1,0:T(8,128)(2,1)} %projections_ref.1, bf16[128,128]{1,0:T(8,128)(2,1)} %output_ref.1), custom_call_target="tpu_custom_call" | custom-call | flops 40000000000 | bytes 4000000 | tf_op jit(solution)/shard_map/attend/pallas_call | solution.py:578
  64.2 1.7 %copy.11 = bf16[8,128,128]{2,1,0:T(8,128)(2,1)} copy(bf16[8,128,128]{2,1,0:T(8,128)(2,1)} %attend.1) | data formatting | bytes 524288
